TPU v7x, 256 devices: a whole 4x4x8 slice. The times are simulated.
256 devices in a mesh: samples: 64 (over z, y, core), groups: 4 (over x).
Axes of the slice: x: 4, y: 4, z: 8, core: 2. Of those that a mesh axis runs over, the one named last changes fastest.
Arguments:
- observed: bfloat16 [1024, 81920], P('samples', 'groups'), may hold values from -200 to 200
- labels: int32 [81920], P('groups'), may hold values from 0 to 255, as said below
- comp_sizes: int32 [256], P('groups'), may hold values from 128 to 512, as said below
Outputs:
- whitened: bfloat16 [1024, 81920], P('samples', 'groups')
Inputs may be any that keep to these rules, and one draw needn't show every extreme that they name: Group g's columns (g * 20480 to (g + 1) * 20480 - 1) carry exactly the labels g * 64 to (g + 1) * 64 - 1, and label c stands on exactly comp_sizes[c] columns. `comp_sizes`: in every group one component has exactly 512 variables; components 2k and 2k + 1 (k = 0, 1, ...) together have exactly 640 variables.
All inputs are finite; a program needn't handle non-finite values. Where the computation divides by a largest or mean magnitude, that divisor is 1e-20 or more.
Results may differ from a plain program's by a relative error of at most 0.0038.
The roundings to bfloat16 on the way count: a program that leaves them out, or rounds other values in their place, can miss the bound.
Values may be sent and summed in bfloat16 or wider, within the bound.
No kernel may reach another device: no remote copies, remote signals or barrier semaphores. Data moves between devices by JAX's collectives and lax.ppermute only.
A program may use at most 64 MiB of HBM per device.

v0:
```python
import functools

import jax
import jax.numpy as jnp
from jax import lax
from jax.experimental import pallas as pl
from jax.experimental.pallas import tpu as pltpu
from jax.sharding import Mesh
from jax.sharding import PartitionSpec as P

CMAX = 512
ITERS = 5
LO = 256
LO_BITS = 8
PLACE_BITS = 10
LANES = 128
CHUNKS = 4
PIECE = 1024
CHIPS = ("samples_0", "samples_1")
SAMPLES = ("samples_0", "samples_1", "samples_2")
BF16 = jnp.bfloat16
F32 = jnp.float32

shrink = 0.2
ridge = 0.5


def iota(shape, axis):
    return lax.broadcasted_iota(jnp.int32, shape, axis)


def dot(a, b, contract=((1,), (0,))):
    return lax.dot_general(a, b, (contract, ((), ())), preferred_element_type=F32)


def halves(x):
    top = x.astype(BF16)
    return top, (x - top.astype(F32)).astype(BF16)


def one_hot_lo(place, ref):
    low = jnp.broadcast_to((place & (LO - 1)).astype(F32), (16, place.shape[1])).astype(BF16)
    level = iota((LO, LANES), 0).astype(F32).astype(BF16)
    for at in range(0, place.shape[1], LANES):
        lanes = slice(at, at + LANES)
        for r in range(0, LO, 16):
            same = level[r : r + 16] == low[:, lanes]
            ref[r : r + 16, lanes] = jnp.where(same, jnp.ones((16, LANES), BF16), jnp.zeros((16, LANES), BF16))


def window_of(begin):
    begin = jnp.concatenate([begin.astype(jnp.int32)] * (LO // LANES), axis=1)
    begin = jnp.broadcast_to(begin, (8, LO))
    return (begin >> LO_BITS) + jnp.where(iota((8, LO), 1) < (begin & (LO - 1)), 1, 0)


def bin_starts(start, bin_row):
    bins = start.shape[0]
    parts = []
    for at in range(0, bin_row.shape[1], LANES):
        same = iota((bins, LANES), 0) == bin_row[:, at : at + LANES]
        parts.append(jnp.sum(jnp.where(same, start, 0.0), axis=0, keepdims=True))
    return jnp.concatenate(parts, axis=1).astype(jnp.int32)


def partition_kernel(slot_ref, labels_ref, x_ref, out_ref, code_ref, start_ref, own_ref, lhs_ref, hot_ref, acc_ref):
    rows, width = x_ref.shape
    chunks, bins = start_ref.shape[0] - 1, start_ref.shape[1]
    chunk = width // chunks
    windows = acc_ref.shape[0]
    bin_width = own_ref.shape[1]
    units = bin_width // LANES
    pair = slot_ref[0] // 2

    label = labels_ref[...] & (2 * bins - 1)
    bin_row = label >> 1
    upper = jnp.where(iota((LO, LO), 0) < iota((LO, LO), 1), 1.0, 0.0)
    counting = jnp.concatenate([upper, jnp.ones((LO, LANES), F32)], axis=1).astype(BF16)
    hots = [iota((bins, LO), 0) == bin_row[:, t : t + LO] for t in range(0, width, LO)]
    ones = jnp.concatenate([jnp.where(hot, 1.0, 0.0).astype(BF16) for hot in hots], axis=0)
    counts = dot(ones, counting)
    done = jnp.zeros((bins, LANES), F32)
    places = []
    most = jnp.zeros((bins, LANES), F32)
    for t, hot in enumerate(hots):
        if t * LO % chunk == 0:
            start_ref[t * LO // chunk] = done
        count = counts[t * bins : (t + 1) * bins]
        inside = jnp.concatenate([done] * (LO // LANES), axis=1) + count[:, :LO]
        places.append(jnp.sum(jnp.where(hot, inside, 0.0), axis=0, keepdims=True))
        done = done + count[:, LO:]
    start_ref[chunks] = done
    for c in range(chunks):
        most = jnp.maximum(most, start_ref[c + 1] - start_ref[c])
    longest = jnp.max(most)
    place = jnp.concatenate(places, axis=1).astype(jnp.int32)
    code_ref[...] = (bin_row << PLACE_BITS) + place

    def masked(c, bin_now, ref):
        columns = slice(c * chunk, (c + 1) * chunk)
        if not isinstance(c, int):
            columns = pl.ds(pl.multiple_of(c * chunk, chunk), chunk)
        x = x_ref[:, columns]
        bin_rows = jnp.broadcast_to(bin_now.astype(F32), (rows, chunk)).astype(BF16)
        for p in range(bins):
            ref[p * rows : (p + 1) * rows, :] = jnp.where(
                bin_rows == jnp.asarray(p, BF16), x, jnp.zeros_like(x)
            )
        mine = jnp.where(bin_now == pair, labels_ref[:, columns] & 1, 0).astype(F32)
        ref[bins * rows :, :] = jnp.broadcast_to(mine, (rows, chunk)).astype(BF16)

    def first_places(c, p):
        if p < bins:
            return start_ref[c, p : p + 1, :]
        return start_ref[c, pl.ds(pair, 1), :]

    runs = []
    for c in range(chunks):
        columns = slice(c * chunk, (c + 1) * chunk)
        one_hot_lo(place[:, columns], hot_ref.at[c])
        masked(c, bin_row[:, columns], lhs_ref.at[c])
        runs.append(dot(lhs_ref[c], hot_ref[c], ((1,), (1,))))

    total = jnp.zeros((8, LANES), F32)
    for at in range(0, width, LANES):
        wide = x_ref[:, at : at + LANES].astype(F32)
        square = wide * wide
        for r in range(0, rows, 8):
            total = total + square[r : r + 8]
    total = whole(total, jnp.sum)
    first = total.astype(BF16).astype(F32)
    second = (total - first).astype(BF16).astype(F32)
    third = total - first - second
    row = iota((8, LANES), 0)
    pieces = jnp.where(row == 0, first, jnp.where(row == 1, second, jnp.where(row == 2, third, 0.0)))
    pieces = pieces.astype(BF16)

    for p in range(bins + 1):
        reached = [window_of(first_places(c, p)) for c in range(chunks)]
        for w in range(windows):
            hits = [window == w for window in reached]
            for half in range(2 if p < bins else 1):
                r = p * rows + half * 8
                value = jnp.where(hits[0], runs[0][r : r + 8], 0.0)
                for hit, run in zip(hits[1:], runs[1:]):
                    value = jnp.where(hit, run[r : r + 8], value)
                for side in range(LO // LANES):
                    u = w * (LO // LANES) + side
                    if u >= units:
                        continue
                    piece = value[:, side * LANES : (side + 1) * LANES]
                    if p < bins:
                        at = half * bin_width + u * LANES
                        out_ref[p, :, at : at + LANES] = piece.astype(BF16)
                    else:
                        own_ref[:, u * LANES : (u + 1) * LANES] = piece
    for p in range(bins):
        out_ref[p, :, 2 * bin_width :] = pieces

    @pl.when(longest > LO)
    def _():
        acc_ref[...] = jnp.zeros_like(acc_ref)
        passes = longest.astype(jnp.int32) // LO + 1

        def one_chunk(c, carry):
            code = code_ref[:, pl.ds(pl.multiple_of(c * chunk, chunk), chunk)]
            now = code >> PLACE_BITS
            code = code & (2**PLACE_BITS - 1)
            turn = (code - bin_starts(start_ref[c], now)) >> LO_BITS

            def one_pass(k, carry):
                masked(c, jnp.where(turn == k, now, -1), lhs_ref.at[0])
                got = dot(lhs_ref[0], hot_ref[c], ((1,), (1,)))
                for p in range(bins + 1):
                    window = window_of(first_places(c, p) + (k * LO).astype(F32))
                    for w in range(windows):
                        for r in range(p * rows, (p + 1) * rows, 8):
                            acc_ref[w, r : r + 8] += jnp.where(window == w, got[r : r + 8], 0.0)
                return carry

            return lax.fori_loop(0, passes, one_pass, carry)

        lax.fori_loop(0, chunks, one_chunk, 0)
        for u in range(units):
            w, side = divmod(u, LO // LANES)
            lanes = slice(side * LANES, (side + 1) * LANES)
            own_ref[:, u * LANES : (u + 1) * LANES] = acc_ref[w, bins * rows : bins * rows + 8, lanes]
            for s in range(2 * bins):
                at = s % 2 * bin_width + u * LANES
                out_ref[s // 2, :, at : at + LANES] = acc_ref[w, s * 8 : s * 8 + 8, lanes].astype(BF16)

    below = jnp.where(iota((LANES, LANES), 0) < iota((LANES, LANES), 1), 1.0, 0.0)
    below = jnp.concatenate([below, jnp.ones((LANES, LANES), F32)], axis=1).astype(BF16)
    so_far = jnp.zeros((8, LANES), F32)
    row = iota((8, LANES), 0)
    for u in range(units):
        lanes = slice(u * LANES, (u + 1) * LANES)
        odds = own_ref[:, lanes]
        count = dot(odds.astype(BF16), below)
        place_odd = so_far + count[:, :LANES]
        place_even = (iota((8, LANES), 1) + u * LANES).astype(F32) - place_odd
        so_far = so_far + count[:, LANES:]
        own_ref[:, lanes] = jnp.where(
            row == 0, jnp.where(odds == 0.0, place_even, -1.0), jnp.where(odds == 1.0, place_odd, -1.0)
        )


def partition(slot, comps, labels, x, chunks=CHUNKS):
    rows, width = x.shape
    bins = comps // 2
    bin_width = width // bins
    windows = -(-bin_width // LO)
    chunk = width // chunks
    outs = [
        jax.ShapeDtypeStruct((bins, rows // 2, 2 * bin_width + LANES), BF16),
        jax.ShapeDtypeStruct((1, width), jnp.int32),
        jax.ShapeDtypeStruct((chunks + 1, bins, LANES), F32),
        jax.ShapeDtypeStruct((8, bin_width), F32),
    ]
    scratch = [
        pltpu.VMEM((chunks, (bins + 1) * rows, chunk), BF16),
        pltpu.VMEM((chunks, LO, chunk), BF16),
        pltpu.VMEM((windows, (bins + 1) * rows, LO), F32),
    ]
    return on_core(partition_kernel, "partition", outs, [slot], [labels.reshape(1, width), x], 48, scratch)


def product(a, b):
    return dot(a[0], b[0]) + (dot(a[0], b[1]) + dot(a[1], b[0]))


def whole(value, reduce):
    return reduce(reduce(value, axis=0, keepdims=True), axis=1, keepdims=True)


def compaction(places_ref, parity):
    place = places_ref[pl.ds(parity, 1), :].astype(jnp.int32)
    return jnp.where(iota((CMAX, places_ref.shape[1]), 0) == place, 1.0, 0.0).astype(BF16)


def groups_of_rows(ref, bin_width):
    for at in (0, bin_width):
        block = ref[:, :, at : at + bin_width]
        yield block.reshape(block.shape[0] * block.shape[1], bin_width)


def gram_kernel(slot_ref, places_ref, own_ref, other_ref, gram_ref, x_ref, energy_ref):
    bin_width = places_ref.shape[1]
    pick = compaction(places_ref, slot_ref[0] % 2)
    total = None
    at = 0
    for ref in (own_ref, other_ref):
        for block in groups_of_rows(ref, bin_width):
            x = dot(block, pick, ((1,), (1,))).astype(BF16)
            if at < x_ref.shape[0]:
                x_ref[at : at + x.shape[0], :] = x
                at += x.shape[0]
            part = dot(x, x, ((0,), (0,)))
            total = part if total is None else total + part
    gram_ref[...] = total
    energy_ref[...] = sum(jnp.sum(ref[:, :, 2 * bin_width :].astype(F32), axis=0) for ref in (own_ref, other_ref))


def powers_kernel(gram_ref, low_ref, high_ref, last_ref, sums_ref, *, row_count):
    covariance = gram_ref[...] * (1.0 / row_count)
    diagonal = iota((CMAX, CMAX), 0) == iota((CMAX, CMAX), 1)
    trace = whole(jnp.where(diagonal, covariance, 0.0), jnp.sum)
    shrunk = (1.0 - shrink) * covariance
    bound = whole(jnp.sum(jnp.abs(shrunk), axis=0, keepdims=True), jnp.max)
    base = jnp.where(diagonal, 1.0, 0.0) - shrunk * (1.0 / jnp.maximum(bound, 1e-30))
    row = iota((8, LANES), 0)
    sums_ref[...] = jnp.where(row == 0, trace, bound)
    for ref in (low_ref, high_ref):
        parts = halves(base)
        square = product(parts, parts)
        squares = halves(square)
        ref[0] = base
        ref[1] = square
        ref[2] = product(squares, parts)
        base = product(squares, squares)
    top, rest = halves(base)
    last_ref[0] = top
    last_ref[1] = rest


def inverse_kernel(slot_ref, sizes_ref, e0_ref, e1_ref, e2_ref, e3_ref, sums_ref, low_ref, high_ref, last_ref, out_ref, *, entries):
    size = sizes_ref[slot_ref[0]]
    energy = e0_ref[...] + e1_ref[...] + e2_ref[...] + e3_ref[...]
    average = (energy[0:1, :1] + energy[1:2, :1] + energy[2:3, :1]) * (1.0 / entries)
    trace, bound = sums_ref[0:1, :1], sums_ref[1:2, :1]
    lift = shrink * (trace / jnp.full((1, 1), size.astype(F32))) + ridge * average
    scale = 1.0 / (bound + lift)
    theta = bound * scale
    diagonal = jnp.where(iota((CMAX, CMAX), 0) == iota((CMAX, CMAX), 1), 1.0, 0.0)
    t2 = theta * theta
    t4 = t2 * t2
    t8 = t4 * t4
    low = diagonal + theta * low_ref[0] + t2 * low_ref[1] + (theta * t2) * low_ref[2]
    high = diagonal + t4 * high_ref[0] + t8 * high_ref[1] + (t4 * t8) * high_ref[2]
    total = product(halves(low), halves(high))
    total = total + (t8 * t8) * product(halves(total), (last_ref[0], last_ref[1]))
    out_ref[...] = (total * scale).astype(BF16)


def whiten_own_kernel(slot_ref, places_ref, rows_ref, x_ref, inverse_ref, done_ref, next_ref):
    parity = slot_ref[0] % 2
    bin_width = places_ref.shape[1]
    mapped = dot(x_ref[...], inverse_ref[...]).astype(BF16)
    done_ref[...] = dot(mapped, compaction(places_ref, parity)).astype(BF16)
    pick = compaction(places_ref, 1 - parity)
    at = 0
    for block in groups_of_rows(rows_ref, bin_width):
        next_ref[at : at + block.shape[0], :] = dot(block, pick, ((1,), (1,))).astype(BF16)
        at += block.shape[0]


def whiten_other_kernel(slot_ref, places_ref, done_ref, x_ref, inverse_ref, out_ref):
    pick = compaction(places_ref, 1 - slot_ref[0] % 2)
    mapped = dot(x_ref[...], inverse_ref[...]).astype(BF16)
    value = (done_ref[...].astype(F32) + dot(mapped, pick)).astype(BF16)
    count, bin_width = value.shape[0] // 2, value.shape[1]
    for half in range(2):
        block = value[half * count : (half + 1) * count].reshape(out_ref.shape[0], out_ref.shape[1], bin_width)
        out_ref[:, :, half * bin_width : (half + 1) * bin_width] = block


def on_core(kernel, name, outs, scalars, arrays, mebibytes, scratch=()):
    def spec(shape):
        return pl.BlockSpec(shape, lambda i: (0,) * len(shape))

    return pl.pallas_call(
        kernel,
        grid=(1,),
        in_specs=[pl.BlockSpec(memory_space=pltpu.SMEM) for _ in scalars] + [spec(a.shape) for a in arrays],
        out_specs=[spec(out.shape) for out in outs],
        out_shape=outs,
        scratch_shapes=list(scratch),
        compiler_params=pltpu.CompilerParams(vmem_limit_bytes=mebibytes << 20),
        name=name,
    )(*scalars, *arrays)


def restore_kernel(code_ref, start_ref, bins_ref, out_ref, mat_ref, lhs_ref, hot_ref):
    bins, half_rows, bin_width = bins_ref.shape
    bin_width = bin_width // 2
    rows, width = out_ref.shape
    slots = 2 * bins
    chunks = start_ref.shape[0] - 1
    chunk = width // chunks
    units = bin_width // LANES
    windows = mat_ref.shape[0]

    for w in range(windows):
        for side in range(LO // LANES):
            u = w * (LO // LANES) + side
            lanes = slice(side * LANES, (side + 1) * LANES)
            for s in range(slots):
                if u < units:
                    at = s % 2 * bin_width + u * LANES
                    piece = bins_ref[s // 2, :, at : at + LANES].astype(F32)
                else:
                    piece = jnp.zeros((half_rows, LANES), F32)
                mat_ref[w, s * half_rows : (s + 1) * half_rows, lanes] = piece
    code = code_ref[...]
    bin_row = code >> PLACE_BITS
    most = start_ref[1] - start_ref[0]
    for c in range(1, chunks):
        most = jnp.maximum(most, start_ref[c + 1] - start_ref[c])
    longest = jnp.max(most)

    def runs(c, shift, ref):
        for p in range(bins):
            window = window_of(start_ref[c, p : p + 1, :] + shift)
            pieces = []
            for r in range(p * rows, (p + 1) * rows, 8):
                value = mat_ref[0, r : r + 8]
                for w in range(1, windows):
                    value = jnp.where(window == w, mat_ref[w, r : r + 8], value)
                pieces.append(value)
            ref[p * rows : (p + 1) * rows] = jnp.concatenate(pieces, axis=0).astype(BF16)

    def choose(lhs, lanes, bin_now, old):
        got = dot(lhs, hot_ref[:, lanes])
        bin_rows = jnp.broadcast_to(bin_now, (8, PIECE))
        for s in range(0, rows, 8):
            value = got[s : s + 8] if old is None else old[s : s + 8]
            for p in range(1 if old is None else 0, bins):
                value = jnp.where(bin_rows == p, got[p * rows + s : p * rows + s + 8], value)
            out_ref[s : s + 8, lanes] = value.astype(BF16)

    for c in range(chunks):
        columns = slice(c * chunk, (c + 1) * chunk)
        one_hot_lo(code[:, columns], hot_ref.at[:, columns])
        runs(c, 0.0, lhs_ref.at[c])
        lhs = lhs_ref[c]
        for at in range(c * chunk, (c + 1) * chunk, PIECE):
            choose(lhs, slice(at, at + PIECE), bin_row[:, at : at + PIECE], None)

    @pl.when(longest > LO)
    def _():
        passes = longest.astype(jnp.int32) // LO + 1

        def one_chunk(c, carry):
            def one_pass(k, carry):
                runs(c, (k * LO).astype(F32), lhs_ref.at[0])

                def one_piece(i, carry):
                    lanes = pl.ds(pl.multiple_of(c * chunk + i * PIECE, PIECE), PIECE)
                    part = code_ref[:, lanes]
                    now = part >> PLACE_BITS
                    turn = ((part & (2**PLACE_BITS - 1)) - bin_starts(start_ref[c], now)) >> LO_BITS
                    choose(lhs_ref[0], lanes, jnp.where(turn == k, now, -1), out_ref[:, lanes].astype(F32))
                    return carry

                return lax.fori_loop(0, chunk // PIECE, one_piece, carry)

            return lax.fori_loop(0, passes, one_pass, carry)

        lax.fori_loop(0, chunks, one_chunk, 0)


def restore(code, start, bins):
    slots, half_rows, bin_width = 2 * bins.shape[0], bins.shape[1], bins.shape[2] // 2
    width = code.shape[1]
    chunks = start.shape[0] - 1
    windows = -(-bin_width // LO)
    scratch = [
        pltpu.VMEM((windows, slots * half_rows, LO), F32),
        pltpu.VMEM((chunks, slots * half_rows, LO), BF16),
        pltpu.VMEM((LO, width), BF16),
    ]
    outs = [jax.ShapeDtypeStruct((2 * half_rows, width), BF16)]
    return on_core(restore_kernel, "restore", outs, [], [code, start, bins], 40, scratch)[0]


def partner(x):
    return lax.ppermute(x, "samples_2", [(0, 1), (1, 0)])


def exchange(x):
    return lax.all_to_all(x, CHIPS, split_axis=0, concat_axis=0, tiled=True)


def body(observed, labels, comp_sizes):
    row_local, width_local = observed.shape
    comps = comp_sizes.shape[0]
    groups = lax.axis_size("groups")
    row_count = row_local * lax.axis_size(SAMPLES)
    bin_width = 2 * width_local // comps
    slot = lax.axis_index(SAMPLES).astype(jnp.int32).reshape(1)
    message, code, start, places = partition(slot, comps, labels, observed)
    rows = exchange(message)
    square = jax.ShapeDtypeStruct((CMAX, CMAX), F32)
    powers = jax.ShapeDtypeStruct((3, CMAX, CMAX), F32)
    narrow = jax.ShapeDtypeStruct((CMAX, CMAX), BF16)
    pair = jax.ShapeDtypeStruct((2, CMAX, CMAX), BF16)
    tall = jax.ShapeDtypeStruct((row_count // 2, CMAX), BF16)
    flat = jax.ShapeDtypeStruct((row_count // 2, bin_width), BF16)
    small = jax.ShapeDtypeStruct((8, LANES), F32)
    back = jax.ShapeDtypeStruct((rows.shape[0], rows.shape[1], 2 * bin_width), BF16)
    gram, x, energy = on_core(
        gram_kernel, "gram", [square, tall, small], [slot], [places, rows, partner(rows)], 16
    )
    energies = [energy] + [
        lax.ppermute(energy, "groups", [(i, (i + k) % groups) for i in range(groups)]) for k in range(1, groups)
    ]
    build = functools.partial(powers_kernel, row_count=row_count)
    low, high, last, sums = on_core(build, "powers", [powers, powers, pair, small], [], [gram], 24)
    finish = functools.partial(inverse_kernel, entries=row_count * width_local * groups)
    (own,) = on_core(
        finish, "inverse", [narrow], [slot, comp_sizes], energies + [sums, low, high, last], 24
    )
    other = partner(own)
    done, waiting = on_core(whiten_own_kernel, "whiten_own", [flat, tall], [slot], [places, rows, x, own], 16)
    (mapped,) = on_core(
        whiten_other_kernel, "whiten_other", [back], [slot], [places, done, waiting, other], 16
    )
    return restore(code, start, exchange(mapped))


def solution(mesh):
    finer = Mesh(
        mesh.devices.reshape(8, 4, 2, mesh.shape["groups"]),
        ("samples_0", "samples_1", "samples_2", "groups"),
    )
    in_specs = (P(SAMPLES, "groups"), P("groups"), P("groups"))
    out_specs = P(SAMPLES, "groups")
    return jax.shard_map(body, mesh=finer, in_specs=in_specs, out_specs=out_specs, check_vma=False)
```

profile of v0, /device:TPU:1, one launch (start us, length us, event | category | flops | bytes accessed | tf_op | source)
XLA Modules:
  0.0 95.9 jit_solution(9465287788034773251)
XLA Ops:
  0.0 0.0 copy-start.2
  0.0 0.0 copy-start
  0.0 1.1 %copy-done = bf16[16,20480]{1,0:T(8,128)(2,1)S(1)} copy-done((bf16[16,20480]{1,0:T(8,128)(2,1)S(1)}, bf16[16,20480]{1,0:T(8,128)(2,1)}, u32[]{:S(2)}) %copy-start) | copy-done | bytes 655384
  1.1 0.9 copy-done.1
  2.0 7.7 %partition.1 = (bf16[32,8,1408]{2,1,0:T(8,128)(2,1)S(1)}, s32[1,20480]{1,0:T(1,128)S(1)}, f32[5,32,128]{2,1,0:T(8,128)S(1)}, f32[8,640]{1,0:T(8,128)S(1)}) custom-call(s32[1]{0:T(128)} %bitcast.slot_ref, s32[1,20480]{1,0:T(1,128)S(1)} %bitcast.2, bf16[16,20480]{1,0:T(8,128)(2,1)S(1)} %copy-done), custom_call_target="tpu_custom_call" | custom-call | tf_op jit(solution)/shard_map/partition/pallas_call | solution.py:331
  9.7 31.8 %all_to_all.10.own_ref.rows_ref = bf16[32,8,1408]{2,1,0:T(8,128)(2,1)S(1)} all-to-all(bf16[32,8,1408]{2,1,0:T(8,128)(2,1)S(1)} %get-tuple-element.21), channel_id=1, replica_groups=mesh['samples_0'=8,'samples_1'=4,'samples_2'=2,'groups'=4] {'samples_0',..., dimensions={0} | all-to-all | bytes 1441792 | tf_op jit(solution)/shard_map/all_to_all | solution.py:441
  41.6 2.7 %collective-permute-start = (bf16[32,8,1408]{2,1,0:T(8,128)(2,1)S(1)}, bf16[32,8,1408]{2,1,0:T(8,128)(2,1)S(1)}, u32[]{:S(2)}, u32[]{:S(2)}) collective-permute-start(bf16[32,8,1408]{2,1,0:T(8,128)(2,1)S(1)} %all_to_all.10.own_ref.rows_ref), channel_id=1, source_target_pairs={{0,4},{4,0},{1,5},{5,1},{2,6},{6,2},{3,7},{7,3},{8,12},{12,8},{9,1... | collective-permute-start | bytes 2162696 | tf_op jit(solution)/shard_map/ppermute | solution.py:437
  44.2 1.8 %collective-permute-done.other_ref = bf16[32,8,1408]{2,1,0:T(8,128)(2,1)S(1)} collective-permute-done((bf16[32,8,1408]{2,1,0:T(8,128)(2,1)S(1)}, bf16[32,8,1408]{2,1,0:T(8,128)(2,1)S(1)}, u32[]{:S(2)}, u32[]{:S(2)}) %collective-permute-start) | collective-permute-done | bytes 720928 | tf_op jit(solution)/shard_map/ppermute | solution.py:437
  46.0 2.1 %gram.1 = (f32[512,512]{1,0:T(8,128)S(1)}, bf16[512,512]{1,0:T(8,128)(2,1)S(1)}, f32[8,128]{1,0:T(8,128)S(1)}) custom-call(s32[1]{0:T(128)} %bitcast.slot_ref, f32[8,640]{1,0:T(8,128)S(1)} %get-tuple-element.20.places_ref, bf16[32,8,1408]{2,1,0:T(8,128)(2,1)S(1)} %all_to_all.10.own_ref.rows_ref, bf16[32,8,1408]{2,1,0:T(8,128)(2,1)S(1)} %collective-permute-done.other_ref), custom_call_target="tpu_custom_call" | custom-call | tf_op jit(solution)/shard_map/gram/pallas_call | solution.py:331
  48.1 1.3 %collective-permute-start.1 = (f32[8,128]{1,0:T(8,128)S(1)}, f32[8,128]{1,0:T(8,128)S(1)}, u32[]{:S(2)}, u32[]{:S(2)}) collective-permute-start(f32[8,128]{1,0:T(8,128)S(1)} %get-tuple-element.23.e0_ref), channel_id=1, source_target_pairs={{0,1},{1,2},{2,3},{3,0},{4,5},{5,6},{6,7},{7,4},{8,9},{9,10},{10,1... | collective-permute-start | bytes 12296 | tf_op jit(solution)/shard_map/ppermute | solution.py:465
  49.4 2.4 %collective-permute-start.2 = (f32[8,128]{1,0:T(8,128)S(1)}, f32[8,128]{1,0:T(8,128)S(1)}, u32[]{:S(2)}, u32[]{:S(2)}) collective-permute-start(f32[8,128]{1,0:T(8,128)S(1)} %get-tuple-element.23.e0_ref), channel_id=1, source_target_pairs={{0,2},{1,3},{2,0},{3,1},{4,6},{5,7},{6,4},{7,5},{8,10},{9,11},{10,... | collective-permute-start | bytes 12296 | tf_op jit(solution)/shard_map/ppermute | solution.py:465
  51.9 1.2 %collective-permute-start.3 = (f32[8,128]{1,0:T(8,128)S(1)}, f32[8,128]{1,0:T(8,128)S(1)}, u32[]{:S(2)}, u32[]{:S(2)}) collective-permute-start(f32[8,128]{1,0:T(8,128)S(1)} %get-tuple-element.23.e0_ref), channel_id=1, source_target_pairs={{0,3},{1,0},{2,1},{3,2},{4,7},{5,4},{6,5},{7,6},{8,11},{9,8},{10,9... | collective-permute-start | bytes 12296 | tf_op jit(solution)/shard_map/ppermute | solution.py:465
  53.0 5.6 %powers.1 = (f32[3,512,512]{2,1,0:T(8,128)S(1)}, f32[3,512,512]{2,1,0:T(8,128)S(1)}, bf16[2,512,512]{2,1,0:T(8,128)(2,1)S(1)}, f32[8,128]{1,0:T(8,128)S(1)}) custom-call(f32[512,512]{1,0:T(8,128)S(1)} %get-tuple-element.24.gram_ref), custom_call_target="tpu_custom_call" | custom-call | tf_op jit(solution)/shard_map/powers/pallas_call | solution.py:331
  58.7 0.0 collective-permute-done.1.e1_ref
  58.7 0.0 collective-permute-done.2.e2_ref
  58.7 0.0 collective-permute-done.3.e3_ref
  58.7 0.0 copy-done.2
  58.7 2.7 %inverse.1.inverse_ref = bf16[512,512]{1,0:T(8,128)(2,1)S(1)} custom-call(s32[1]{0:T(128)} %bitcast.slot_ref, s32[64]{0:T(128)S(1)} %copy-done.2, f32[8,128]{1,0:T(8,128)S(1)} %get-tuple-element.23.e0_ref, f32[8,128]{1,0:T(8,128)S(1)} %collective-permute-done.1.e1_ref, f32[8,128]{1,0:T(8,128)S(1)} %collective-permute-done.2.e2_ref, ...), custom_call_target="tpu_custom_call" | custom-call | tf_op jit(solution)/shard_map/inverse/pallas_call | solution.py:331
  61.4 1.3 %collective-permute-start.4 = (bf16[512,512]{1,0:T(8,128)(2,1)S(1)}, bf16[512,512]{1,0:T(8,128)(2,1)S(1)}, u32[]{:S(2)}, u32[]{:S(2)}) collective-permute-start(bf16[512,512]{1,0:T(8,128)(2,1)S(1)} %inverse.1.inverse_ref), channel_id=1, source_target_pairs={{0,4},{4,0},{1,5},{5,1},{2,6},{6,2},{3,7},{7,3},{8,12},{12,8},{9,1... | collective-permute-start | bytes 1572872 | tf_op jit(solution)/shard_map/ppermute | solution.py:437
  62.7 1.3 %whiten_own.1 = (bf16[512,640]{1,0:T(8,128)(2,1)S(1)}, bf16[512,512]{1,0:T(8,128)(2,1)S(1)}) custom-call(s32[1]{0:T(128)} %bitcast.slot_ref, f32[8,640]{1,0:T(8,128)S(1)} %get-tuple-element.20.places_ref, bf16[32,8,1408]{2,1,0:T(8,128)(2,1)S(1)} %all_to_all.10.own_ref.rows_ref, bf16[512,512]{1,0:T(8,128)(2,1)S(1)} %get-tuple-element.22.x_ref, ...), custom_call_target="tpu_custom_call" | custom-call | tf_op jit(solution)/shard_map/whiten_own/pallas_call | solution.py:331
  64.1 0.2 collective-permute-done.4.inverse_ref
  64.3 0.9 whiten_other.1
  65.1 23.2 %all_to_all.11.bins_ref = bf16[32,8,1280]{2,1,0:T(8,128)(2,1)S(1)} all-to-all(bf16[32,8,1280]{2,1,0:T(8,128)(2,1)S(1)} %whiten_other.1), channel_id=1, replica_groups=mesh['samples_0'=8,'samples_1'=4,'samples_2'=2,'groups'=4] {'samples_0',..., dimensions={0} | all-to-all | bytes 1310720 | tf_op jit(solution)/shard_map/all_to_all | solution.py:441
  88.3 7.6 %restore.1 = bf16[16,20480]{1,0:T(8,128)(2,1)} custom-call(s32[1,20480]{1,0:T(1,128)S(1)} %get-tuple-element.18.code_ref, f32[5,32,128]{2,1,0:T(8,128)S(1)} %get-tuple-element.19.start_ref, bf16[32,8,1280]{2,1,0:T(8,128)(2,1)S(1)} %all_to_all.11.bins_ref), custom_call_target="tpu_custom_call" | custom-call | tf_op jit(solution)/shard_map/restore/pallas_call | solution.py:331
  (1 shorter events, 0.0 us)
Async XLA Ops:
  0.0 58.7 %copy-start.2 = (s32[64]{0:T(128)S(1)}, s32[64]{0:T(128)}, u32[]{:S(2)}) copy-start(s32[64]{0:T(128)} %sizes_ref.1) | copy-start | bytes 772
  0.0 1.1 %copy-start = (bf16[16,20480]{1,0:T(8,128)(2,1)S(1)}, bf16[16,20480]{1,0:T(8,128)(2,1)}, u32[]{:S(2)}) copy-start(bf16[16,20480]{1,0:T(8,128)(2,1)} %x_ref.1) | copy-start | bytes 1966084
  1.1 0.9 copy-start.1
  41.6 4.5 %collective-permute-start = (bf16[32,8,1408]{2,1,0:T(8,128)(2,1)S(1)}, bf16[32,8,1408]{2,1,0:T(8,128)(2,1)S(1)}, u32[]{:S(2)}, u32[]{:S(2)}) collective-permute-start(bf16[32,8,1408]{2,1,0:T(8,128)(2,1)S(1)} %all_to_all.10.own_ref.rows_ref), channel_id=1, source_target_pairs={{0,4},{4,0},{1,5},{5,1},{2,6},{6,2},{3,7},{7,3},{8,12},{12,8},{9,1... | collective-permute-start | bytes 2162696 | tf_op jit(solution)/shard_map/ppermute | solution.py:437
  48.1 10.5 %collective-permute-start.1 = (f32[8,128]{1,0:T(8,128)S(1)}, f32[8,128]{1,0:T(8,128)S(1)}, u32[]{:S(2)}, u32[]{:S(2)}) collective-permute-start(f32[8,128]{1,0:T(8,128)S(1)} %get-tuple-element.23.e0_ref), channel_id=1, source_target_pairs={{0,1},{1,2},{2,3},{3,0},{4,5},{5,6},{6,7},{7,4},{8,9},{9,10},{10,1... | collective-permute-start | bytes 12296 | tf_op jit(solution)/shard_map/ppermute | solution.py:465
  49.4 9.3 %collective-permute-start.2 = (f32[8,128]{1,0:T(8,128)S(1)}, f32[8,128]{1,0:T(8,128)S(1)}, u32[]{:S(2)}, u32[]{:S(2)}) collective-permute-start(f32[8,128]{1,0:T(8,128)S(1)} %get-tuple-element.23.e0_ref), channel_id=1, source_target_pairs={{0,2},{1,3},{2,0},{3,1},{4,6},{5,7},{6,4},{7,5},{8,10},{9,11},{10,... | collective-permute-start | bytes 12296 | tf_op jit(solution)/shard_map/ppermute | solution.py:465
  51.9 6.8 %collective-permute-start.3 = (f32[8,128]{1,0:T(8,128)S(1)}, f32[8,128]{1,0:T(8,128)S(1)}, u32[]{:S(2)}, u32[]{:S(2)}) collective-permute-start(f32[8,128]{1,0:T(8,128)S(1)} %get-tuple-element.23.e0_ref), channel_id=1, source_target_pairs={{0,3},{1,0},{2,1},{3,2},{4,7},{5,4},{6,5},{7,6},{8,11},{9,8},{10,9... | collective-permute-start | bytes 12296 | tf_op jit(solution)/shard_map/ppermute | solution.py:465
  61.4 2.8 %collective-permute-start.4 = (bf16[512,512]{1,0:T(8,128)(2,1)S(1)}, bf16[512,512]{1,0:T(8,128)(2,1)S(1)}, u32[]{:S(2)}, u32[]{:S(2)}) collective-permute-start(bf16[512,512]{1,0:T(8,128)(2,1)S(1)} %inverse.1.inverse_ref), channel_id=1, source_target_pairs={{0,4},{4,0},{1,5},{5,1},{2,6},{6,2},{3,7},{7,3},{8,12},{12,8},{9,1... | collective-permute-start | bytes 1572872 | tf_op jit(solution)/shard_map/ppermute | solution.py:437
where the time goes:
time: 96.7 us; the launch traced here: 95.9 us
  blocking collectives  55 us (57%)
  Pallas kernels  27.9 us (29%)
  starting transfers between devices  8.86 us (9%)
  waiting for transfers between devices  2.04 us (2%)
  local copies, waits for them, and re-layouts  1.99 us (2%)
    all_to_all x2, blocking collectives, exchange(): return lax.all_to_all(x, CHIPS, split_axis=0, concat_axis=0, tiled=True)  55 us
    pallas_call x7, Pallas kernels, on_core(): pl.pallas_call(kernel, grid=(1,), in_specs=[pl.BlockSpec(memory_space=plt...  27.9 us
    ppermute x3, starting transfers between devices, body(): lax.ppermute(energy, 'groups', [(i, (i + k) % groups) for i in range(grou...  4.9 us
    ppermute x2, starting transfers between devices, partner(): return lax.ppermute(x, 'samples_2', [(0, 1), (1, 0)])  3.96 us
    ppermute x2, waiting for transfers between devices, partner(): return lax.ppermute(x, 'samples_2', [(0, 1), (1, 0)])  2.03 us
    unnamed x6, local copies, waits for them, and re-layouts  1.99 us
  transfers between devices with their start and end apart: 5, of which 2 were waited for; matrix products, arithmetic and copies ran while one was open for 0% of the time, Pallas kernels for 7%

commit v1 on v0

--- a/solution.py
+++ b/solution.py
@@ -63,15 +63,10 @@
     return jnp.concatenate(parts, axis=1).astype(jnp.int32)
 
 
-def partition_kernel(slot_ref, labels_ref, x_ref, out_ref, code_ref, start_ref, own_ref, lhs_ref, hot_ref, acc_ref):
-    rows, width = x_ref.shape
+def places_kernel(labels_ref, code_ref, start_ref):
+    width = labels_ref.shape[1]
     chunks, bins = start_ref.shape[0] - 1, start_ref.shape[1]
     chunk = width // chunks
-    windows = acc_ref.shape[0]
-    bin_width = own_ref.shape[1]
-    units = bin_width // LANES
-    pair = slot_ref[0] // 2
-
     label = labels_ref[...] & (2 * bins - 1)
     bin_row = label >> 1
     upper = jnp.where(iota((LO, LO), 0) < iota((LO, LO), 1), 1.0, 0.0)
@@ -81,7 +76,6 @@
     counts = dot(ones, counting)
     done = jnp.zeros((bins, LANES), F32)
     places = []
-    most = jnp.zeros((bins, LANES), F32)
     for t, hot in enumerate(hots):
         if t * LO % chunk == 0:
             start_ref[t * LO // chunk] = done
@@ -90,11 +84,37 @@
         places.append(jnp.sum(jnp.where(hot, inside, 0.0), axis=0, keepdims=True))
         done = done + count[:, LO:]
     start_ref[chunks] = done
-    for c in range(chunks):
+    place = jnp.concatenate(places, axis=1).astype(jnp.int32)
+    code_ref[...] = (label << PLACE_BITS) + place
+
+
+def places_of(comps, labels, chunks=CHUNKS):
+    width = labels.shape[0]
+    outs = [
+        jax.ShapeDtypeStruct((1, width), jnp.int32),
+        jax.ShapeDtypeStruct((chunks + 1, comps // 2, LANES), F32),
+    ]
+    return on_core(places_kernel, "places", outs, [], [labels.reshape(1, width)], 16, work=2 * 10**9)
+
+
+def longest_run(start_ref):
+    most = start_ref[1] - start_ref[0]
+    for c in range(1, start_ref.shape[0] - 1):
         most = jnp.maximum(most, start_ref[c + 1] - start_ref[c])
-    longest = jnp.max(most)
-    place = jnp.concatenate(places, axis=1).astype(jnp.int32)
-    code_ref[...] = (bin_row << PLACE_BITS) + place
+    return jnp.max(most)
+
+
+def partition_kernel(slot_ref, code_ref, start_ref, x_ref, out_ref, own_ref, hot_ref, lhs_ref, acc_ref):
+    rows, width = x_ref.shape
+    chunks, bins = start_ref.shape[0] - 1, start_ref.shape[1]
+    chunk = width // chunks
+    windows = acc_ref.shape[0]
+    bin_width = own_ref.shape[1]
+    units = bin_width // LANES
+    pair = slot_ref[0] // 2
+    bin_row = code_ref[...] >> (PLACE_BITS + 1)
+    place = code_ref[...] & (2**PLACE_BITS - 1)
+    longest = longest_run(start_ref)
 
     def masked(c, bin_now, ref):
         columns = slice(c * chunk, (c + 1) * chunk)
@@ -106,7 +126,7 @@
             ref[p * rows : (p + 1) * rows, :] = jnp.where(
                 bin_rows == jnp.asarray(p, BF16), x, jnp.zeros_like(x)
             )
-        mine = jnp.where(bin_now == pair, labels_ref[:, columns] & 1, 0).astype(F32)
+        mine = jnp.where(bin_now == pair, (code_ref[:, columns] >> PLACE_BITS) & 1, 0).astype(F32)
         ref[bins * rows :, :] = jnp.broadcast_to(mine, (rows, chunk)).astype(BF16)
 
     def first_places(c, p):
@@ -164,7 +184,7 @@
 
         def one_chunk(c, carry):
             code = code_ref[:, pl.ds(pl.multiple_of(c * chunk, chunk), chunk)]
-            now = code >> PLACE_BITS
+            now = code >> (PLACE_BITS + 1)
             code = code & (2**PLACE_BITS - 1)
             turn = (code - bin_starts(start_ref[c], now)) >> LO_BITS
 
@@ -205,24 +225,23 @@
         )
 
 
-def partition(slot, comps, labels, x, chunks=CHUNKS):
+def partition(slot, code, start, x):
     rows, width = x.shape
-    bins = comps // 2
+    chunks, bins = start.shape[0] - 1, start.shape[1]
     bin_width = width // bins
     windows = -(-bin_width // LO)
     chunk = width // chunks
     outs = [
         jax.ShapeDtypeStruct((bins, rows // 2, 2 * bin_width + LANES), BF16),
-        jax.ShapeDtypeStruct((1, width), jnp.int32),
-        jax.ShapeDtypeStruct((chunks + 1, bins, LANES), F32),
         jax.ShapeDtypeStruct((8, bin_width), F32),
+        jax.ShapeDtypeStruct((chunks, LO, chunk), BF16),
     ]
     scratch = [
         pltpu.VMEM((chunks, (bins + 1) * rows, chunk), BF16),
-        pltpu.VMEM((chunks, LO, chunk), BF16),
         pltpu.VMEM((windows, (bins + 1) * rows, LO), F32),
     ]
-    return on_core(partition_kernel, "partition", outs, [slot], [labels.reshape(1, width), x], 48, scratch)
+    inputs = [code, start, x]
+    return on_core(partition_kernel, "partition", outs, [slot], inputs, 38, scratch)
 
 
 def product(a, b):
@@ -244,21 +263,29 @@
         yield block.reshape(block.shape[0] * block.shape[1], bin_width)
 
 
-def gram_kernel(slot_ref, places_ref, own_ref, other_ref, gram_ref, x_ref, energy_ref):
+def energy_of(ref, bin_width):
+    return jnp.sum(ref[:, :, 2 * bin_width :].astype(F32), axis=0)
+
+
+def gram_own_kernel(slot_ref, places_ref, rows_ref, gram_ref, x_ref, energy_ref):
     bin_width = places_ref.shape[1]
     pick = compaction(places_ref, slot_ref[0] % 2)
-    total = None
     at = 0
-    for ref in (own_ref, other_ref):
-        for block in groups_of_rows(ref, bin_width):
-            x = dot(block, pick, ((1,), (1,))).astype(BF16)
-            if at < x_ref.shape[0]:
-                x_ref[at : at + x.shape[0], :] = x
-                at += x.shape[0]
-            part = dot(x, x, ((0,), (0,)))
-            total = part if total is None else total + part
-    gram_ref[...] = total
-    energy_ref[...] = sum(jnp.sum(ref[:, :, 2 * bin_width :].astype(F32), axis=0) for ref in (own_ref, other_ref))
+    for block in groups_of_rows(rows_ref, bin_width):
+        x_ref[at : at + block.shape[0], :] = dot(block, pick, ((1,), (1,))).astype(BF16)
+        at += block.shape[0]
+    x = x_ref[...]
+    gram_ref[...] = dot(x, x, ((0,), (0,)))
+    energy_ref[...] = energy_of(rows_ref, bin_width)
+
+
+def gram_other_kernel(slot_ref, places_ref, rows_ref, before_ref, energy_before_ref, gram_ref, energy_ref):
+    bin_width = places_ref.shape[1]
+    pick = compaction(places_ref, slot_ref[0] % 2)
+    blocks = [dot(block, pick, ((1,), (1,))).astype(BF16) for block in groups_of_rows(rows_ref, bin_width)]
+    x = jnp.concatenate(blocks, axis=0)
+    gram_ref[...] = before_ref[...] + dot(x, x, ((0,), (0,)))
+    energy_ref[...] = energy_before_ref[...] + energy_of(rows_ref, bin_width)
 
 
 def powers_kernel(gram_ref, low_ref, high_ref, last_ref, sums_ref, *, row_count):
@@ -324,7 +351,7 @@
         out_ref[:, :, half * bin_width : (half + 1) * bin_width] = block
 
 
-def on_core(kernel, name, outs, scalars, arrays, mebibytes, scratch=()):
+def on_core(kernel, name, outs, scalars, arrays, mebibytes, scratch=(), work=None):
     def spec(shape):
         return pl.BlockSpec(shape, lambda i: (0,) * len(shape))
 
@@ -336,11 +363,12 @@
         out_shape=outs,
         scratch_shapes=list(scratch),
         compiler_params=pltpu.CompilerParams(vmem_limit_bytes=mebibytes << 20),
+        cost_estimate=work and pl.CostEstimate(flops=work, bytes_accessed=1 << 17, transcendentals=0),
         name=name,
     )(*scalars, *arrays)
 
 
-def restore_kernel(code_ref, start_ref, bins_ref, out_ref, mat_ref, lhs_ref, hot_ref):
+def restore_kernel(code_ref, start_ref, hot_ref, bins_ref, out_ref, mat_ref, lhs_ref):
     bins, half_rows, bin_width = bins_ref.shape
     bin_width = bin_width // 2
     rows, width = out_ref.shape
@@ -362,11 +390,8 @@
                     piece = jnp.zeros((half_rows, LANES), F32)
                 mat_ref[w, s * half_rows : (s + 1) * half_rows, lanes] = piece
     code = code_ref[...]
-    bin_row = code >> PLACE_BITS
-    most = start_ref[1] - start_ref[0]
-    for c in range(1, chunks):
-        most = jnp.maximum(most, start_ref[c + 1] - start_ref[c])
-    longest = jnp.max(most)
+    bin_row = code >> (PLACE_BITS + 1)
+    longest = longest_run(start_ref)
 
     def runs(c, shift, ref):
         for p in range(bins):
@@ -379,8 +404,8 @@
                 pieces.append(value)
             ref[p * rows : (p + 1) * rows] = jnp.concatenate(pieces, axis=0).astype(BF16)
 
-    def choose(lhs, lanes, bin_now, old):
-        got = dot(lhs, hot_ref[:, lanes])
+    def choose(lhs, hot, lanes, bin_now, old):
+        got = dot(lhs, hot)
         bin_rows = jnp.broadcast_to(bin_now, (8, PIECE))
         for s in range(0, rows, 8):
             value = got[s : s + 8] if old is None else old[s : s + 8]
@@ -389,12 +414,11 @@
             out_ref[s : s + 8, lanes] = value.astype(BF16)
 
     for c in range(chunks):
-        columns = slice(c * chunk, (c + 1) * chunk)
-        one_hot_lo(code[:, columns], hot_ref.at[:, columns])
         runs(c, 0.0, lhs_ref.at[c])
         lhs = lhs_ref[c]
-        for at in range(c * chunk, (c + 1) * chunk, PIECE):
-            choose(lhs, slice(at, at + PIECE), bin_row[:, at : at + PIECE], None)
+        for at in range(0, chunk, PIECE):
+            lanes = slice(c * chunk + at, c * chunk + at + PIECE)
+            choose(lhs, hot_ref[c, :, at : at + PIECE], lanes, bin_row[:, lanes], None)
 
     @pl.when(longest > LO)
     def _():
@@ -407,9 +431,10 @@
                 def one_piece(i, carry):
                     lanes = pl.ds(pl.multiple_of(c * chunk + i * PIECE, PIECE), PIECE)
                     part = code_ref[:, lanes]
-                    now = part >> PLACE_BITS
+                    now = part >> (PLACE_BITS + 1)
                     turn = ((part & (2**PLACE_BITS - 1)) - bin_starts(start_ref[c], now)) >> LO_BITS
-                    choose(lhs_ref[0], lanes, jnp.where(turn == k, now, -1), out_ref[:, lanes].astype(F32))
+                    hot = hot_ref[c, :, pl.ds(pl.multiple_of(i * PIECE, PIECE), PIECE)]
+                    choose(lhs_ref[0], hot, lanes, jnp.where(turn == k, now, -1), out_ref[:, lanes].astype(F32))
                     return carry
 
                 return lax.fori_loop(0, chunk // PIECE, one_piece, carry)
@@ -419,7 +444,7 @@
         lax.fori_loop(0, chunks, one_chunk, 0)
 
 
-def restore(code, start, bins):
+def restore(code, start, hot, bins):
     slots, half_rows, bin_width = 2 * bins.shape[0], bins.shape[1], bins.shape[2] // 2
     width = code.shape[1]
     chunks = start.shape[0] - 1
@@ -427,10 +452,9 @@
     scratch = [
         pltpu.VMEM((windows, slots * half_rows, LO), F32),
         pltpu.VMEM((chunks, slots * half_rows, LO), BF16),
-        pltpu.VMEM((LO, width), BF16),
     ]
     outs = [jax.ShapeDtypeStruct((2 * half_rows, width), BF16)]
-    return on_core(restore_kernel, "restore", outs, [], [code, start, bins], 40, scratch)[0]
+    return on_core(restore_kernel, "restore", outs, [], [code, start, hot, bins], 28, scratch)[0]
 
 
 def partner(x):
@@ -448,7 +472,8 @@
     row_count = row_local * lax.axis_size(SAMPLES)
     bin_width = 2 * width_local // comps
     slot = lax.axis_index(SAMPLES).astype(jnp.int32).reshape(1)
-    message, code, start, places = partition(slot, comps, labels, observed)
+    code, start = places_of(comps, labels)
+    message, places, hot = partition(slot, code, start, observed)
     rows = exchange(message)
     square = jax.ShapeDtypeStruct((CMAX, CMAX), F32)
     powers = jax.ShapeDtypeStruct((3, CMAX, CMAX), F32)
@@ -458,8 +483,10 @@
     flat = jax.ShapeDtypeStruct((row_count // 2, bin_width), BF16)
     small = jax.ShapeDtypeStruct((8, LANES), F32)
     back = jax.ShapeDtypeStruct((rows.shape[0], rows.shape[1], 2 * bin_width), BF16)
-    gram, x, energy = on_core(
-        gram_kernel, "gram", [square, tall, small], [slot], [places, rows, partner(rows)], 16
+    others = partner(rows)
+    gram, x, energy = on_core(gram_own_kernel, "gram_own", [square, tall, small], [slot], [places, rows], 12)
+    gram, energy = on_core(
+        gram_other_kernel, "gram_other", [square, small], [slot], [places, others, gram, energy], 12
     )
     energies = [energy] + [
         lax.ppermute(energy, "groups", [(i, (i + k) % groups) for i in range(groups)]) for k in range(1, groups)
@@ -475,7 +502,7 @@
     (mapped,) = on_core(
         whiten_other_kernel, "whiten_other", [back], [slot], [places, done, waiting, other], 16
     )
-    return restore(code, start, exchange(mapped))
+    return restore(code, start, hot, exchange(mapped))
 
 
 def solution(mesh):

time: 96.7 us -> 94.1 us (0.973)
  local copies, waits for them, and re-layouts: 1.99 us -> 0.96 us
    unnamed x6, local copies, waits for them, and re-layouts: 1.99 us -> 0.96 us
    pallas_call x7 -> x9, Pallas kernels: 27.9 us -> 27.1 us  [on_core(): pl.pallas_call(kernel, grid=(1,), in_specs=[pl.BlockSpec(memory_space=plt...]
  transfers between devices with their start and end apart: 5 -> 5, of which waited for: 2 -> 2; matrix products, arithmetic and copies ran while one was open for 0% -> 0% of each run, Pallas kernels for 7% -> 8%
where the time goes in v1:
time: 94.1 us; the launch traced here: 93.3 us
  blocking collectives  55 us (58%)
  Pallas kernels  27.1 us (29%)
  starting transfers between devices  9.04 us (10%)
  waiting for transfers between devices  1.11 us (1%)
  local copies, waits for them, and re-layouts  0.96 us (1%)
    all_to_all x2, blocking collectives, exchange(): return lax.all_to_all(x, CHIPS, split_axis=0, concat_axis=0, tiled=True)  55 us
    pallas_call x9, Pallas kernels, on_core(): pl.pallas_call(kernel, grid=(1,), in_specs=[pl.BlockSpec(memory_space=plt...  27.1 us
    ppermute x3, starting transfers between devices, body(): lax.ppermute(energy, 'groups', [(i, (i + k) % groups) for i in range(grou...  5.08 us
    ppermute x2, starting transfers between devices, partner(): return lax.ppermute(x, 'samples_2', [(0, 1), (1, 0)])  3.97 us
  transfers between devices with their start and end apart: 5, of which 2 were waited for; matrix products, arithmetic and copies ran while one was open for 0% of the time, Pallas kernels for 8%

profile of v1, /device:TPU:1, one launch (start us, length us, event | category | flops | bytes accessed | tf_op | source)
XLA Modules:
  0.0 93.3 jit_solution(12934875208775760953)
XLA Ops:
  0.0 0.9 copy-done.2
  0.9 1.0 %places.1 = (s32[1,20480]{1,0:T(1,128)S(1)}, f32[5,32,128]{2,1,0:T(8,128)S(1)}) custom-call(s32[1,20480]{1,0:T(1,128)S(1)} %bitcast.2), custom_call_target="tpu_custom_call" | custom-call | flops 2000000000 | bytes 131072 | tf_op jit(solution)/shard_map/places/pallas_call | solution.py:358
  1.9 0.0 copy-start.1
  1.9 0.1 copy-done
  2.0 7.1 %partition.1 = (bf16[32,8,1408]{2,1,0:T(8,128)(2,1)S(1)}, f32[8,640]{1,0:T(8,128)S(1)}, bf16[4,256,5120]{2,1,0:T(8,128)(2,1)S(1)}) custom-call(s32[1]{0:T(128)} %bitcast.1.slot_ref, s32[1,20480]{1,0:T(1,128)S(1)} %get-tuple-element.21.code_ref, f32[5,32,128]{2,1,0:T(8,128)S(1)} %get-tuple-element.22.start_ref, bf16[16,20480]{1,0:T(8,128)(2,1)S(1)} %copy-done), custom_call_target="tpu_custom_call" | custom-call | tf_op jit(solution)/shard_map/partition/pallas_call | solution.py:358
  9.1 31.8 %all_to_all.10.rows_ref = bf16[32,8,1408]{2,1,0:T(8,128)(2,1)S(1)} all-to-all(bf16[32,8,1408]{2,1,0:T(8,128)(2,1)S(1)} %get-tuple-element.25), channel_id=1, replica_groups=mesh['samples_0'=8,'samples_1'=4,'samples_2'=2,'groups'=4] {'samples_0',..., dimensions={0} | all-to-all | bytes 1441792 | tf_op jit(solution)/shard_map/all_to_all | solution.py:465
  40.9 2.7 %collective-permute-start = (bf16[32,8,1408]{2,1,0:T(8,128)(2,1)S(1)}, bf16[32,8,1408]{2,1,0:T(8,128)(2,1)S(1)}, u32[]{:S(2)}, u32[]{:S(2)}) collective-permute-start(bf16[32,8,1408]{2,1,0:T(8,128)(2,1)S(1)} %all_to_all.10.rows_ref), channel_id=1, source_target_pairs={{0,4},{4,0},{1,5},{5,1},{2,6},{6,2},{3,7},{7,3},{8,12},{12,8},{9,1... | collective-permute-start | bytes 2162696 | tf_op jit(solution)/shard_map/ppermute | solution.py:461
  43.6 0.9 gram_own.1
  44.5 0.9 collective-permute-done.rows_ref
  45.4 0.9 gram_other.1
  46.3 1.5 %collective-permute-start.1 = (f32[8,128]{1,0:T(8,128)S(1)}, f32[8,128]{1,0:T(8,128)S(1)}, u32[]{:S(2)}, u32[]{:S(2)}) collective-permute-start(f32[8,128]{1,0:T(8,128)S(1)} %get-tuple-element.29.e0_ref), channel_id=1, source_target_pairs={{0,1},{1,2},{2,3},{3,0},{4,5},{5,6},{6,7},{7,4},{8,9},{9,10},{10,1... | collective-permute-start | bytes 12296 | tf_op jit(solution)/shard_map/ppermute | solution.py:492
  47.8 2.5 %collective-permute-start.2 = (f32[8,128]{1,0:T(8,128)S(1)}, f32[8,128]{1,0:T(8,128)S(1)}, u32[]{:S(2)}, u32[]{:S(2)}) collective-permute-start(f32[8,128]{1,0:T(8,128)S(1)} %get-tuple-element.29.e0_ref), channel_id=1, source_target_pairs={{0,2},{1,3},{2,0},{3,1},{4,6},{5,7},{6,4},{7,5},{8,10},{9,11},{10,... | collective-permute-start | bytes 12296 | tf_op jit(solution)/shard_map/ppermute | solution.py:492
  50.2 1.2 %collective-permute-start.3 = (f32[8,128]{1,0:T(8,128)S(1)}, f32[8,128]{1,0:T(8,128)S(1)}, u32[]{:S(2)}, u32[]{:S(2)}) collective-permute-start(f32[8,128]{1,0:T(8,128)S(1)} %get-tuple-element.29.e0_ref), channel_id=1, source_target_pairs={{0,3},{1,0},{2,1},{3,2},{4,7},{5,4},{6,5},{7,6},{8,11},{9,8},{10,9... | collective-permute-start | bytes 12296 | tf_op jit(solution)/shard_map/ppermute | solution.py:492
  51.4 5.6 %powers.1 = (f32[3,512,512]{2,1,0:T(8,128)S(1)}, f32[3,512,512]{2,1,0:T(8,128)S(1)}, bf16[2,512,512]{2,1,0:T(8,128)(2,1)S(1)}, f32[8,128]{1,0:T(8,128)S(1)}) custom-call(f32[512,512]{1,0:T(8,128)S(1)} %get-tuple-element.30.gram_ref), custom_call_target="tpu_custom_call" | custom-call | tf_op jit(solution)/shard_map/powers/pallas_call | solution.py:358
  57.0 0.0 collective-permute-done.1.e1_ref
  57.0 0.0 collective-permute-done.2.e2_ref
  57.0 0.0 collective-permute-done.3.e3_ref
  57.1 2.7 %inverse.1.inverse_ref = bf16[512,512]{1,0:T(8,128)(2,1)S(1)} custom-call(s32[1]{0:T(128)} %bitcast.1.slot_ref, s32[64]{0:T(128)S(1)} %copy-done.1, f32[8,128]{1,0:T(8,128)S(1)} %get-tuple-element.29.e0_ref, f32[8,128]{1,0:T(8,128)S(1)} %collective-permute-done.1.e1_ref, f32[8,128]{1,0:T(8,128)S(1)} %collective-permute-done.2.e2_ref, ...), custom_call_target="tpu_custom_call" | custom-call | tf_op jit(solution)/shard_map/inverse/pallas_call | solution.py:358
  59.8 1.3 %collective-permute-start.4 = (bf16[512,512]{1,0:T(8,128)(2,1)S(1)}, bf16[512,512]{1,0:T(8,128)(2,1)S(1)}, u32[]{:S(2)}, u32[]{:S(2)}) collective-permute-start(bf16[512,512]{1,0:T(8,128)(2,1)S(1)} %inverse.1.inverse_ref), channel_id=1, source_target_pairs={{0,4},{4,0},{1,5},{5,1},{2,6},{6,2},{3,7},{7,3},{8,12},{12,8},{9,1... | collective-permute-start | bytes 1572872 | tf_op jit(solution)/shard_map/ppermute | solution.py:461
  61.1 1.3 %whiten_own.1 = (bf16[512,640]{1,0:T(8,128)(2,1)S(1)}, bf16[512,512]{1,0:T(8,128)(2,1)S(1)}) custom-call(s32[1]{0:T(128)} %bitcast.1.slot_ref, f32[8,640]{1,0:T(8,128)S(1)} %get-tuple-element.24.places_ref, bf16[32,8,1408]{2,1,0:T(8,128)(2,1)S(1)} %all_to_all.10.rows_ref, bf16[512,512]{1,0:T(8,128)(2,1)S(1)} %get-tuple-element.26.x_ref, ...), custom_call_target="tpu_custom_call" | custom-call | tf_op jit(solution)/shard_map/whiten_own/pallas_call | solution.py:358
  62.4 0.2 collective-permute-done.4.inverse_ref
  62.6 0.9 whiten_other.1
  63.5 23.2 %all_to_all.11.bins_ref = bf16[32,8,1280]{2,1,0:T(8,128)(2,1)S(1)} all-to-all(bf16[32,8,1280]{2,1,0:T(8,128)(2,1)S(1)} %whiten_other.1), channel_id=1, replica_groups=mesh['samples_0'=8,'samples_1'=4,'samples_2'=2,'groups'=4] {'samples_0',..., dimensions={0} | all-to-all | bytes 1310720 | tf_op jit(solution)/shard_map/all_to_all | solution.py:465
  86.7 6.6 %restore.1 = bf16[16,20480]{1,0:T(8,128)(2,1)} custom-call(s32[1,20480]{1,0:T(1,128)S(1)} %get-tuple-element.21.code_ref, f32[5,32,128]{2,1,0:T(8,128)S(1)} %get-tuple-element.22.start_ref, bf16[4,256,5120]{2,1,0:T(8,128)(2,1)S(1)} %get-tuple-element.23.hot_ref, bf16[32,8,1280]{2,1,0:T(8,128)(2,1)S(1)} %all_to_all.11.bins_ref), custom_call_target="tpu_custom_call" | custom-call | tf_op jit(solution)/shard_map/restore/pallas_call | solution.py:358
  (3 shorter events, 0.0 us)
Async XLA Ops:
  0.0 0.9 copy-start.2
  0.9 1.1 %copy-start = (bf16[16,20480]{1,0:T(8,128)(2,1)S(1)}, bf16[16,20480]{1,0:T(8,128)(2,1)}, u32[]{:S(2)}) copy-start(bf16[16,20480]{1,0:T(8,128)(2,1)} %x_ref.1) | copy-start | bytes 1966084
  1.9 55.2 %copy-start.1 = (s32[64]{0:T(128)S(1)}, s32[64]{0:T(128)}, u32[]{:S(2)}) copy-start(s32[64]{0:T(128)} %sizes_ref.1) | copy-start | bytes 772
  40.9 4.5 %collective-permute-start = (bf16[32,8,1408]{2,1,0:T(8,128)(2,1)S(1)}, bf16[32,8,1408]{2,1,0:T(8,128)(2,1)S(1)}, u32[]{:S(2)}, u32[]{:S(2)}) collective-permute-start(bf16[32,8,1408]{2,1,0:T(8,128)(2,1)S(1)} %all_to_all.10.rows_ref), channel_id=1, source_target_pairs={{0,4},{4,0},{1,5},{5,1},{2,6},{6,2},{3,7},{7,3},{8,12},{12,8},{9,1... | collective-permute-start | bytes 2162696 | tf_op jit(solution)/shard_map/ppermute | solution.py:461
  46.3 10.7 %collective-permute-start.1 = (f32[8,128]{1,0:T(8,128)S(1)}, f32[8,128]{1,0:T(8,128)S(1)}, u32[]{:S(2)}, u32[]{:S(2)}) collective-permute-start(f32[8,128]{1,0:T(8,128)S(1)} %get-tuple-element.29.e0_ref), channel_id=1, source_target_pairs={{0,1},{1,2},{2,3},{3,0},{4,5},{5,6},{6,7},{7,4},{8,9},{9,10},{10,1... | collective-permute-start | bytes 12296 | tf_op jit(solution)/shard_map/ppermute | solution.py:492
  47.8 9.3 %collective-permute-start.2 = (f32[8,128]{1,0:T(8,128)S(1)}, f32[8,128]{1,0:T(8,128)S(1)}, u32[]{:S(2)}, u32[]{:S(2)}) collective-permute-start(f32[8,128]{1,0:T(8,128)S(1)} %get-tuple-element.29.e0_ref), channel_id=1, source_target_pairs={{0,2},{1,3},{2,0},{3,1},{4,6},{5,7},{6,4},{7,5},{8,10},{9,11},{10,... | collective-permute-start | bytes 12296 | tf_op jit(solution)/shard_map/ppermute | solution.py:492
  50.2 6.8 %collective-permute-start.3 = (f32[8,128]{1,0:T(8,128)S(1)}, f32[8,128]{1,0:T(8,128)S(1)}, u32[]{:S(2)}, u32[]{:S(2)}) collective-permute-start(f32[8,128]{1,0:T(8,128)S(1)} %get-tuple-element.29.e0_ref), channel_id=1, source_target_pairs={{0,3},{1,0},{2,1},{3,2},{4,7},{5,4},{6,5},{7,6},{8,11},{9,8},{10,9... | collective-permute-start | bytes 12296 | tf_op jit(solution)/shard_map/ppermute | solution.py:492
  59.8 2.8 %collective-permute-start.4 = (bf16[512,512]{1,0:T(8,128)(2,1)S(1)}, bf16[512,512]{1,0:T(8,128)(2,1)S(1)}, u32[]{:S(2)}, u32[]{:S(2)}) collective-permute-start(bf16[512,512]{1,0:T(8,128)(2,1)S(1)} %inverse.1.inverse_ref), channel_id=1, source_target_pairs={{0,4},{4,0},{1,5},{5,1},{2,6},{6,2},{3,7},{7,3},{8,12},{12,8},{9,1... | collective-permute-start | bytes 1572872 | tf_op jit(solution)/shard_map/ppermute | solution.py:461

commit v2 on v1

--- a/solution.py
+++ b/solution.py
@@ -94,7 +94,7 @@
         jax.ShapeDtypeStruct((1, width), jnp.int32),
         jax.ShapeDtypeStruct((chunks + 1, comps // 2, LANES), F32),
     ]
-    return on_core(places_kernel, "places", outs, [], [labels.reshape(1, width)], 16, work=2 * 10**9)
+    return on_core(places_kernel, "places", outs, [], [labels.reshape(1, width)], 16, work=8 * 10**9)
 
 
 def longest_run(start_ref):
@@ -288,7 +288,7 @@
     energy_ref[...] = energy_before_ref[...] + energy_of(rows_ref, bin_width)
 
 
-def powers_kernel(gram_ref, low_ref, high_ref, last_ref, sums_ref, *, row_count):
+def first_powers_kernel(gram_ref, low_ref, fourth_ref, sums_ref, *, row_count):
     covariance = gram_ref[...] * (1.0 / row_count)
     diagonal = iota((CMAX, CMAX), 0) == iota((CMAX, CMAX), 1)
     trace = whole(jnp.where(diagonal, covariance, 0.0), jnp.sum)
@@ -297,22 +297,34 @@
     base = jnp.where(diagonal, 1.0, 0.0) - shrunk * (1.0 / jnp.maximum(bound, 1e-30))
     row = iota((8, LANES), 0)
     sums_ref[...] = jnp.where(row == 0, trace, bound)
-    for ref in (low_ref, high_ref):
-        parts = halves(base)
-        square = product(parts, parts)
-        squares = halves(square)
-        ref[0] = base
-        ref[1] = square
-        ref[2] = product(squares, parts)
-        base = product(squares, squares)
-    top, rest = halves(base)
+    parts = halves(base)
+    square = product(parts, parts)
+    squares = halves(square)
+    low_ref[0] = base
+    low_ref[1] = square
+    low_ref[2] = product(squares, parts)
+    fourth_ref[...] = product(squares, squares)
+
+
+def eighth_power_kernel(fourth_ref, energy_ref, neighbour_ref, eighth_ref, sum_ref):
+    parts = halves(fourth_ref[...])
+    eighth_ref[...] = product(parts, parts)
+    sum_ref[...] = energy_ref[...] + neighbour_ref[...]
+
+
+def last_powers_kernel(fourth_ref, eighth_ref, twelfth_ref, last_ref):
+    parts = halves(eighth_ref[...])
+    twelfth_ref[...] = product(parts, halves(fourth_ref[...]))
+    top, rest = halves(product(parts, parts))
     last_ref[0] = top
     last_ref[1] = rest
 
 
-def inverse_kernel(slot_ref, sizes_ref, e0_ref, e1_ref, e2_ref, e3_ref, sums_ref, low_ref, high_ref, last_ref, out_ref, *, entries):
+def inverse_kernel(
+    slot_ref, sizes_ref, e0_ref, e1_ref, sums_ref, low_ref, fourth_ref, eighth_ref, twelfth_ref, last_ref, out_ref, *, entries
+):
     size = sizes_ref[slot_ref[0]]
-    energy = e0_ref[...] + e1_ref[...] + e2_ref[...] + e3_ref[...]
+    energy = e0_ref[...] + e1_ref[...]
     average = (energy[0:1, :1] + energy[1:2, :1] + energy[2:3, :1]) * (1.0 / entries)
     trace, bound = sums_ref[0:1, :1], sums_ref[1:2, :1]
     lift = shrink * (trace / jnp.full((1, 1), size.astype(F32))) + ridge * average
@@ -323,7 +335,7 @@
     t4 = t2 * t2
     t8 = t4 * t4
     low = diagonal + theta * low_ref[0] + t2 * low_ref[1] + (theta * t2) * low_ref[2]
-    high = diagonal + t4 * high_ref[0] + t8 * high_ref[1] + (t4 * t8) * high_ref[2]
+    high = diagonal + t4 * fourth_ref[...] + t8 * eighth_ref[...] + (t4 * t8) * twelfth_ref[...]
     total = product(halves(low), halves(high))
     total = total + (t8 * t8) * product(halves(total), (last_ref[0], last_ref[1]))
     out_ref[...] = (total * scale).astype(BF16)
@@ -459,6 +471,10 @@
 
 def partner(x):
     return lax.ppermute(x, "samples_2", [(0, 1), (1, 0)])
+
+
+def across(x, apart):
+    return lax.ppermute(x, "groups", [(i, i ^ apart) for i in range(lax.axis_size("groups"))])
 
 
 def exchange(x):
@@ -488,14 +504,22 @@
     gram, energy = on_core(
         gram_other_kernel, "gram_other", [square, small], [slot], [places, others, gram, energy], 12
     )
-    energies = [energy] + [
-        lax.ppermute(energy, "groups", [(i, (i + k) % groups) for i in range(groups)]) for k in range(1, groups)
-    ]
-    build = functools.partial(powers_kernel, row_count=row_count)
-    low, high, last, sums = on_core(build, "powers", [powers, powers, pair, small], [], [gram], 24)
+    neighbour = across(energy, 1)
+    build = functools.partial(first_powers_kernel, row_count=row_count)
+    low, fourth, sums = on_core(build, "first_powers", [powers, square, small], [], [gram], 16)
+    eighth, energy = on_core(
+        eighth_power_kernel, "eighth_power", [square, small], [], [fourth, energy, neighbour], 12
+    )
+    others = across(energy, 2)
+    twelfth, last = on_core(last_powers_kernel, "last_powers", [square, pair], [], [fourth, eighth], 16)
     finish = functools.partial(inverse_kernel, entries=row_count * width_local * groups)
     (own,) = on_core(
-        finish, "inverse", [narrow], [slot, comp_sizes], energies + [sums, low, high, last], 24
+        finish,
+        "inverse",
+        [narrow],
+        [slot, comp_sizes],
+        [energy, others, sums, low, fourth, eighth, twelfth, last],
+        24,
     )
     other = partner(own)
     done, waiting = on_core(whiten_own_kernel, "whiten_own", [flat, tall], [slot], [places, rows, x, own], 16)

time: 94.1 us -> 93.7 us (level)
    ppermute x3 -> x2, starting transfers between devices: 5.08 us -> 4.02 us  [across(): lax.ppermute(x, 'groups', [(i, i ^ apart) for i in range(lax.axis_size('g...]
    pallas_call x9 -> x11, Pallas kernels: 27.1 us -> 27.5 us  [on_core(): pl.pallas_call(kernel, grid=(1,), in_specs=[pl.BlockSpec(memory_space=plt...]
  transfers between devices with their start and end apart: 5 -> 4, of which waited for: 2 -> 2; matrix products, arithmetic and copies ran while one was open for 0% -> 0% of each run, Pallas kernels for 8% -> 8%
where the time goes in v2:
time: 93.7 us; the launch traced here: 92.9 us
  blocking collectives  55 us (59%)
  Pallas kernels  27.5 us (29%)
  starting transfers between devices  8.23 us (9%)
  waiting for transfers between devices  1.11 us (1%)
  local copies, waits for them, and re-layouts  0.97 us (1%)
    all_to_all x2, blocking collectives, exchange(): return lax.all_to_all(x, CHIPS, split_axis=0, concat_axis=0, tiled=True)  55 us
    pallas_call x11, Pallas kernels, on_core(): pl.pallas_call(kernel, grid=(1,), in_specs=[pl.BlockSpec(memory_space=plt...  27.5 us
    ppermute x2, starting transfers between devices, partner(): return lax.ppermute(x, 'samples_2', [(0, 1), (1, 0)])  4.21 us
    ppermute x2, starting transfers between devices, across(): lax.ppermute(x, 'groups', [(i, i ^ apart) for i in range(lax.axis_size('g...  4.02 us
  transfers between devices with their start and end apart: 4, of which 2 were waited for; matrix products, arithmetic and copies ran while one was open for 0% of the time, Pallas kernels for 8%

profile of v2, /device:TPU:1, one launch (start us, length us, event | category | flops | bytes accessed | tf_op | source)
XLA Modules:
  0.0 92.9 jit_solution(17463989529007997548)
XLA Ops:
  0.0 0.9 copy-done.2
  0.9 1.0 %places.1 = (s32[1,20480]{1,0:T(1,128)S(1)}, f32[5,32,128]{2,1,0:T(8,128)S(1)}) custom-call(s32[1,20480]{1,0:T(1,128)S(1)} %bitcast.2), custom_call_target="tpu_custom_call" | custom-call | flops 8000000000 | bytes 131072 | tf_op jit(solution)/shard_map/places/pallas_call | solution.py:370
  1.9 0.1 copy-done
  2.0 7.1 %partition.1 = (bf16[32,8,1408]{2,1,0:T(8,128)(2,1)S(1)}, f32[8,640]{1,0:T(8,128)S(1)}, bf16[4,256,5120]{2,1,0:T(8,128)(2,1)S(1)}) custom-call(s32[1]{0:T(128)} %bitcast.1.slot_ref, s32[1,20480]{1,0:T(1,128)S(1)} %get-tuple-element.24.code_ref, f32[5,32,128]{2,1,0:T(8,128)S(1)} %get-tuple-element.25.start_ref, bf16[16,20480]{1,0:T(8,128)(2,1)S(1)} %copy-done), custom_call_target="tpu_custom_call" | custom-call | tf_op jit(solution)/shard_map/partition/pallas_call | solution.py:370
  9.1 31.8 %all_to_all.10.rows_ref = bf16[32,8,1408]{2,1,0:T(8,128)(2,1)S(1)} all-to-all(bf16[32,8,1408]{2,1,0:T(8,128)(2,1)S(1)} %get-tuple-element.28), channel_id=1, replica_groups=mesh['samples_0'=8,'samples_1'=4,'samples_2'=2,'groups'=4] {'samples_0',..., dimensions={0} | all-to-all | bytes 1441792 | tf_op jit(solution)/shard_map/all_to_all | solution.py:481
  40.9 2.7 %collective-permute-start = (bf16[32,8,1408]{2,1,0:T(8,128)(2,1)S(1)}, bf16[32,8,1408]{2,1,0:T(8,128)(2,1)S(1)}, u32[]{:S(2)}, u32[]{:S(2)}) collective-permute-start(bf16[32,8,1408]{2,1,0:T(8,128)(2,1)S(1)} %all_to_all.10.rows_ref), channel_id=1, source_target_pairs={{0,4},{4,0},{1,5},{5,1},{2,6},{6,2},{3,7},{7,3},{8,12},{12,8},{9,1... | collective-permute-start | bytes 2162696 | tf_op jit(solution)/shard_map/ppermute | solution.py:473
  43.6 0.9 gram_own.1
  44.5 0.9 collective-permute-done.rows_ref
  45.4 0.9 gram_other.1
  46.3 1.5 %collective-permute-start.1 = (f32[8,128]{1,0:T(8,128)S(1)}, f32[8,128]{1,0:T(8,128)S(1)}, u32[]{:S(2)}, u32[]{:S(2)}) collective-permute-start(f32[8,128]{1,0:T(8,128)S(1)} %get-tuple-element.34.energy_ref), channel_id=1, source_target_pairs={{0,1},{1,0},{2,3},{3,2},{4,5},{5,4},{6,7},{7,6},{8,9},{9,8},{10,11... | collective-permute-start | bytes 12296 | tf_op jit(solution)/shard_map/ppermute | solution.py:477
  47.8 3.1 %first_powers.1 = (f32[3,512,512]{2,1,0:T(8,128)S(1)}, f32[512,512]{1,0:T(8,128)S(1)}, f32[8,128]{1,0:T(8,128)S(1)}) custom-call(f32[512,512]{1,0:T(8,128)S(1)} %get-tuple-element.32.gram_ref), custom_call_target="tpu_custom_call" | custom-call | tf_op jit(solution)/shard_map/first_powers/pallas_call | solution.py:370
  50.9 0.0 collective-permute-done.1.neighbour_ref
  50.9 1.0 %eighth_power.1 = (f32[512,512]{1,0:T(8,128)S(1)}, f32[8,128]{1,0:T(8,128)S(1)}) custom-call(f32[512,512]{1,0:T(8,128)S(1)} %get-tuple-element.33.fourth_ref, f32[8,128]{1,0:T(8,128)S(1)} %get-tuple-element.34.energy_ref, f32[8,128]{1,0:T(8,128)S(1)} %collective-permute-done.1.neighbour_ref), custom_call_target="tpu_custom_call" | custom-call | tf_op jit(solution)/shard_map/eighth_power/pallas_call | solution.py:370
  51.9 2.5 %collective-permute-start.2 = (f32[8,128]{1,0:T(8,128)S(1)}, f32[8,128]{1,0:T(8,128)S(1)}, u32[]{:S(2)}, u32[]{:S(2)}) collective-permute-start(f32[8,128]{1,0:T(8,128)S(1)} %get-tuple-element.35.e0_ref), channel_id=1, source_target_pairs={{0,2},{1,3},{2,0},{3,1},{4,6},{5,7},{6,4},{7,5},{8,10},{9,11},{10,... | collective-permute-start | bytes 12296 | tf_op jit(solution)/shard_map/ppermute | solution.py:477
  54.4 1.8 %last_powers.1 = (f32[512,512]{1,0:T(8,128)S(1)}, bf16[2,512,512]{2,1,0:T(8,128)(2,1)S(1)}) custom-call(f32[512,512]{1,0:T(8,128)S(1)} %get-tuple-element.33.fourth_ref, f32[512,512]{1,0:T(8,128)S(1)} %get-tuple-element.38.eighth_ref), custom_call_target="tpu_custom_call" | custom-call | tf_op jit(solution)/shard_map/last_powers/pallas_call | solution.py:370
  56.3 0.0 collective-permute-done.2.e1_ref
  56.3 0.0 copy-done.1
  56.3 2.8 %inverse.1.inverse_ref = bf16[512,512]{1,0:T(8,128)(2,1)S(1)} custom-call(s32[1]{0:T(128)} %bitcast.1.slot_ref, s32[64]{0:T(128)S(1)} %copy-done.1, f32[8,128]{1,0:T(8,128)S(1)} %get-tuple-element.35.e0_ref, f32[8,128]{1,0:T(8,128)S(1)} %collective-permute-done.2.e1_ref, f32[8,128]{1,0:T(8,128)S(1)} %get-tuple-element.36.sums_ref, ...), custom_call_target="tpu_custom_call" | custom-call | tf_op jit(solution)/shard_map/inverse/pallas_call | solution.py:370
  59.1 1.5 %collective-permute-start.3 = (bf16[512,512]{1,0:T(8,128)(2,1)S(1)}, bf16[512,512]{1,0:T(8,128)(2,1)S(1)}, u32[]{:S(2)}, u32[]{:S(2)}) collective-permute-start(bf16[512,512]{1,0:T(8,128)(2,1)S(1)} %inverse.1.inverse_ref), channel_id=1, source_target_pairs={{0,4},{4,0},{1,5},{5,1},{2,6},{6,2},{3,7},{7,3},{8,12},{12,8},{9,1... | collective-permute-start | bytes 1572872 | tf_op jit(solution)/shard_map/ppermute | solution.py:473
  60.6 1.3 %whiten_own.1 = (bf16[512,640]{1,0:T(8,128)(2,1)S(1)}, bf16[512,512]{1,0:T(8,128)(2,1)S(1)}) custom-call(s32[1]{0:T(128)} %bitcast.1.slot_ref, f32[8,640]{1,0:T(8,128)S(1)} %get-tuple-element.27.places_ref, bf16[32,8,1408]{2,1,0:T(8,128)(2,1)S(1)} %all_to_all.10.rows_ref, bf16[512,512]{1,0:T(8,128)(2,1)S(1)} %get-tuple-element.29.x_ref, ...), custom_call_target="tpu_custom_call" | custom-call | tf_op jit(solution)/shard_map/whiten_own/pallas_call | solution.py:370
  61.9 0.2 collective-permute-done.3.inverse_ref
  62.2 0.9 whiten_other.1
  63.0 23.2 %all_to_all.11.bins_ref = bf16[32,8,1280]{2,1,0:T(8,128)(2,1)S(1)} all-to-all(bf16[32,8,1280]{2,1,0:T(8,128)(2,1)S(1)} %whiten_other.1), channel_id=1, replica_groups=mesh['samples_0'=8,'samples_1'=4,'samples_2'=2,'groups'=4] {'samples_0',..., dimensions={0} | all-to-all | bytes 1310720 | tf_op jit(solution)/shard_map/all_to_all | solution.py:481
  86.2 6.6 %restore.1 = bf16[16,20480]{1,0:T(8,128)(2,1)} custom-call(s32[1,20480]{1,0:T(1,128)S(1)} %get-tuple-element.24.code_ref, f32[5,32,128]{2,1,0:T(8,128)S(1)} %get-tuple-element.25.start_ref, bf16[4,256,5120]{2,1,0:T(8,128)(2,1)S(1)} %get-tuple-element.26.hot_ref, bf16[32,8,1280]{2,1,0:T(8,128)(2,1)S(1)} %all_to_all.11.bins_ref), custom_call_target="tpu_custom_call" | custom-call | tf_op jit(solution)/shard_map/restore/pallas_call | solution.py:370
  (3 shorter events, 0.0 us)
Async XLA Ops:
  0.0 0.9 copy-start.2
  0.9 1.1 %copy-start = (bf16[16,20480]{1,0:T(8,128)(2,1)S(1)}, bf16[16,20480]{1,0:T(8,128)(2,1)}, u32[]{:S(2)}) copy-start(bf16[16,20480]{1,0:T(8,128)(2,1)} %x_ref.1) | copy-start | bytes 1966084
  0.9 55.4 %copy-start.1 = (s32[64]{0:T(128)S(1)}, s32[64]{0:T(128)}, u32[]{:S(2)}) copy-start(s32[64]{0:T(128)} %sizes_ref.1) | copy-start | bytes 772
  40.9 4.5 %collective-permute-start = (bf16[32,8,1408]{2,1,0:T(8,128)(2,1)S(1)}, bf16[32,8,1408]{2,1,0:T(8,128)(2,1)S(1)}, u32[]{:S(2)}, u32[]{:S(2)}) collective-permute-start(bf16[32,8,1408]{2,1,0:T(8,128)(2,1)S(1)} %all_to_all.10.rows_ref), channel_id=1, source_target_pairs={{0,4},{4,0},{1,5},{5,1},{2,6},{6,2},{3,7},{7,3},{8,12},{12,8},{9,1... | collective-permute-start | bytes 2162696 | tf_op jit(solution)/shard_map/ppermute | solution.py:473
  46.3 4.6 %collective-permute-start.1 = (f32[8,128]{1,0:T(8,128)S(1)}, f32[8,128]{1,0:T(8,128)S(1)}, u32[]{:S(2)}, u32[]{:S(2)}) collective-permute-start(f32[8,128]{1,0:T(8,128)S(1)} %get-tuple-element.34.energy_ref), channel_id=1, source_target_pairs={{0,1},{1,0},{2,3},{3,2},{4,5},{5,4},{6,7},{7,6},{8,9},{9,8},{10,11... | collective-permute-start | bytes 12296 | tf_op jit(solution)/shard_map/ppermute | solution.py:477
  51.9 4.4 %collective-permute-start.2 = (f32[8,128]{1,0:T(8,128)S(1)}, f32[8,128]{1,0:T(8,128)S(1)}, u32[]{:S(2)}, u32[]{:S(2)}) collective-permute-start(f32[8,128]{1,0:T(8,128)S(1)} %get-tuple-element.35.e0_ref), channel_id=1, source_target_pairs={{0,2},{1,3},{2,0},{3,1},{4,6},{5,7},{6,4},{7,5},{8,10},{9,11},{10,... | collective-permute-start | bytes 12296 | tf_op jit(solution)/shard_map/ppermute | solution.py:477
  59.1 3.1 %collective-permute-start.3 = (bf16[512,512]{1,0:T(8,128)(2,1)S(1)}, bf16[512,512]{1,0:T(8,128)(2,1)S(1)}, u32[]{:S(2)}, u32[]{:S(2)}) collective-permute-start(bf16[512,512]{1,0:T(8,128)(2,1)S(1)} %inverse.1.inverse_ref), channel_id=1, source_target_pairs={{0,4},{4,0},{1,5},{5,1},{2,6},{6,2},{3,7},{7,3},{8,12},{12,8},{9,1... | collective-permute-start | bytes 1572872 | tf_op jit(solution)/shard_map/ppermute | solution.py:473

commit v3 on v2

--- a/solution.py
+++ b/solution.py
@@ -244,8 +244,16 @@
     return on_core(partition_kernel, "partition", outs, [slot], inputs, 38, scratch)
 
 
+def passes(a, b):
+    return dot(a[0], b[0]) + (dot(a[0], b[1]) + dot(a[1], b[0]))
+
+
 def product(a, b):
-    return dot(a[0], b[0]) + (dot(a[0], b[1]) + dot(a[1], b[0]))
+    half = CMAX // 2
+    top = passes([x[:half] for x in a], b)
+    corner = passes([x[half:] for x in a], [x[:, half:] for x in b])
+    bottom = jnp.concatenate([jnp.transpose(top[:, half:]), corner], axis=1)
+    return jnp.concatenate([top, bottom], axis=0)
 
 
 def whole(value, reduce):

time: 93.7 us -> 92.8 us (level)
  Pallas kernels: 27.5 us -> 26.2 us
    pallas_call x11, Pallas kernels: 27.5 us -> 26.2 us  [on_core(): pl.pallas_call(kernel, grid=(1,), in_specs=[pl.BlockSpec(memory_space=plt...]
  transfers between devices with their start and end apart: 4 -> 4, of which waited for: 2 -> 2; matrix products, arithmetic and copies ran while one was open for 0% -> 0% of each run, Pallas kernels for 8% -> 7%
where the time goes in v3:
time: 92.8 us; the launch traced here: 92 us
  blocking collectives  55 us (59%)
  Pallas kernels  26.2 us (28%)
  starting transfers between devices  8.56 us (9%)
  waiting for transfers between devices  1.11 us (1%)
  local copies, waits for them, and re-layouts  0.97 us (1%)
    all_to_all x2, blocking collectives, exchange(): return lax.all_to_all(x, CHIPS, split_axis=0, concat_axis=0, tiled=True)  55 us
    pallas_call x11, Pallas kernels, on_core(): pl.pallas_call(kernel, grid=(1,), in_specs=[pl.BlockSpec(memory_space=plt...  26.2 us
    ppermute x2, starting transfers between devices, partner(): return lax.ppermute(x, 'samples_2', [(0, 1), (1, 0)])  4.54 us
    ppermute x2, starting transfers between devices, across(): lax.ppermute(x, 'groups', [(i, i ^ apart) for i in range(lax.axis_size('g...  4.02 us
  transfers between devices with their start and end apart: 4, of which 2 were waited for; matrix products, arithmetic and copies ran while one was open for 0% of the time, Pallas kernels for 7%

profile of v3, /device:TPU:1, one launch (start us, length us, event | category | flops | bytes accessed | tf_op | source)
XLA Modules:
  0.0 92.0 jit_solution(5142285462485577751)
XLA Ops:
  0.0 0.9 copy-done.2
  0.9 1.0 %places.1 = (s32[1,20480]{1,0:T(1,128)S(1)}, f32[5,32,128]{2,1,0:T(8,128)S(1)}) custom-call(s32[1,20480]{1,0:T(1,128)S(1)} %bitcast.2), custom_call_target="tpu_custom_call" | custom-call | flops 8000000000 | bytes 131072 | tf_op jit(solution)/shard_map/places/pallas_call | solution.py:378
  1.9 0.1 copy-done
  2.0 7.1 %partition.1 = (bf16[32,8,1408]{2,1,0:T(8,128)(2,1)S(1)}, f32[8,640]{1,0:T(8,128)S(1)}, bf16[4,256,5120]{2,1,0:T(8,128)(2,1)S(1)}) custom-call(s32[1]{0:T(128)} %bitcast.1.slot_ref, s32[1,20480]{1,0:T(1,128)S(1)} %get-tuple-element.24.code_ref, f32[5,32,128]{2,1,0:T(8,128)S(1)} %get-tuple-element.25.start_ref, bf16[16,20480]{1,0:T(8,128)(2,1)S(1)} %copy-done), custom_call_target="tpu_custom_call" | custom-call | tf_op jit(solution)/shard_map/partition/pallas_call | solution.py:378
  9.1 31.8 %all_to_all.10.rows_ref = bf16[32,8,1408]{2,1,0:T(8,128)(2,1)S(1)} all-to-all(bf16[32,8,1408]{2,1,0:T(8,128)(2,1)S(1)} %get-tuple-element.28), channel_id=1, replica_groups=mesh['samples_0'=8,'samples_1'=4,'samples_2'=2,'groups'=4] {'samples_0',..., dimensions={0} | all-to-all | bytes 1441792 | tf_op jit(solution)/shard_map/all_to_all | solution.py:489
  40.9 2.7 %collective-permute-start = (bf16[32,8,1408]{2,1,0:T(8,128)(2,1)S(1)}, bf16[32,8,1408]{2,1,0:T(8,128)(2,1)S(1)}, u32[]{:S(2)}, u32[]{:S(2)}) collective-permute-start(bf16[32,8,1408]{2,1,0:T(8,128)(2,1)S(1)} %all_to_all.10.rows_ref), channel_id=1, source_target_pairs={{0,4},{4,0},{1,5},{5,1},{2,6},{6,2},{3,7},{7,3},{8,12},{12,8},{9,1... | collective-permute-start | bytes 2162696 | tf_op jit(solution)/shard_map/ppermute | solution.py:481
  43.6 0.9 %gram_own.1 = (f32[512,512]{1,0:T(8,128)S(1)}, bf16[512,512]{1,0:T(8,128)(2,1)S(1)}, f32[8,128]{1,0:T(8,128)S(1)}) custom-call(s32[1]{0:T(128)} %bitcast.1.slot_ref, f32[8,640]{1,0:T(8,128)S(1)} %get-tuple-element.27.places_ref, bf16[32,8,1408]{2,1,0:T(8,128)(2,1)S(1)} %all_to_all.10.rows_ref), custom_call_target="tpu_custom_call" | custom-call | tf_op jit(solution)/shard_map/gram_own/pallas_call | solution.py:378
  44.5 0.9 collective-permute-done.rows_ref
  45.4 0.9 %gram_other.1 = (f32[512,512]{1,0:T(8,128)S(1)}, f32[8,128]{1,0:T(8,128)S(1)}) custom-call(s32[1]{0:T(128)} %bitcast.1.slot_ref, f32[8,640]{1,0:T(8,128)S(1)} %get-tuple-element.27.places_ref, bf16[32,8,1408]{2,1,0:T(8,128)(2,1)S(1)} %collective-permute-done.rows_ref, f32[512,512]{1,0:T(8,128)S(1)} %get-tuple-element.30.before_ref, ...), custom_call_target="tpu_custom_call" | custom-call | tf_op jit(solution)/shard_map/gram_other/pallas_call | solution.py:378
  46.3 1.5 %collective-permute-start.1 = (f32[8,128]{1,0:T(8,128)S(1)}, f32[8,128]{1,0:T(8,128)S(1)}, u32[]{:S(2)}, u32[]{:S(2)}) collective-permute-start(f32[8,128]{1,0:T(8,128)S(1)} %get-tuple-element.34.energy_ref), channel_id=1, source_target_pairs={{0,1},{1,0},{2,3},{3,2},{4,5},{5,4},{6,7},{7,6},{8,9},{9,8},{10,11... | collective-permute-start | bytes 12296 | tf_op jit(solution)/shard_map/ppermute | solution.py:485
  47.8 2.6 %first_powers.1 = (f32[3,512,512]{2,1,0:T(8,128)S(1)}, f32[512,512]{1,0:T(8,128)S(1)}, f32[8,128]{1,0:T(8,128)S(1)}) custom-call(f32[512,512]{1,0:T(8,128)S(1)} %get-tuple-element.32.gram_ref), custom_call_target="tpu_custom_call" | custom-call | tf_op jit(solution)/shard_map/first_powers/pallas_call | solution.py:378
  50.4 0.0 collective-permute-done.1.neighbour_ref
  50.4 0.9 eighth_power.1
  51.3 2.5 %collective-permute-start.2 = (f32[8,128]{1,0:T(8,128)S(1)}, f32[8,128]{1,0:T(8,128)S(1)}, u32[]{:S(2)}, u32[]{:S(2)}) collective-permute-start(f32[8,128]{1,0:T(8,128)S(1)} %get-tuple-element.35.e0_ref), channel_id=1, source_target_pairs={{0,2},{1,3},{2,0},{3,1},{4,6},{5,7},{6,4},{7,5},{8,10},{9,11},{10,... | collective-permute-start | bytes 12296 | tf_op jit(solution)/shard_map/ppermute | solution.py:485
  53.8 1.5 %last_powers.1 = (f32[512,512]{1,0:T(8,128)S(1)}, bf16[2,512,512]{2,1,0:T(8,128)(2,1)S(1)}) custom-call(f32[512,512]{1,0:T(8,128)S(1)} %get-tuple-element.33.fourth_ref, f32[512,512]{1,0:T(8,128)S(1)} %get-tuple-element.38.eighth_ref), custom_call_target="tpu_custom_call" | custom-call | tf_op jit(solution)/shard_map/last_powers/pallas_call | solution.py:378
  55.3 0.0 collective-permute-done.2.e1_ref
  55.3 0.0 copy-done.1
  55.3 2.5 %inverse.1.inverse_ref = bf16[512,512]{1,0:T(8,128)(2,1)S(1)} custom-call(s32[1]{0:T(128)} %bitcast.1.slot_ref, s32[64]{0:T(128)S(1)} %copy-done.1, f32[8,128]{1,0:T(8,128)S(1)} %get-tuple-element.35.e0_ref, f32[8,128]{1,0:T(8,128)S(1)} %collective-permute-done.2.e1_ref, f32[8,128]{1,0:T(8,128)S(1)} %get-tuple-element.36.sums_ref, ...), custom_call_target="tpu_custom_call" | custom-call | tf_op jit(solution)/shard_map/inverse/pallas_call | solution.py:378
  57.8 1.9 %collective-permute-start.3 = (bf16[512,512]{1,0:T(8,128)(2,1)S(1)}, bf16[512,512]{1,0:T(8,128)(2,1)S(1)}, u32[]{:S(2)}, u32[]{:S(2)}) collective-permute-start(bf16[512,512]{1,0:T(8,128)(2,1)S(1)} %inverse.1.inverse_ref), channel_id=1, source_target_pairs={{0,4},{4,0},{1,5},{5,1},{2,6},{6,2},{3,7},{7,3},{8,12},{12,8},{9,1... | collective-permute-start | bytes 1572872 | tf_op jit(solution)/shard_map/ppermute | solution.py:481
  59.7 1.3 %whiten_own.1 = (bf16[512,640]{1,0:T(8,128)(2,1)S(1)}, bf16[512,512]{1,0:T(8,128)(2,1)S(1)}) custom-call(s32[1]{0:T(128)} %bitcast.1.slot_ref, f32[8,640]{1,0:T(8,128)S(1)} %get-tuple-element.27.places_ref, bf16[32,8,1408]{2,1,0:T(8,128)(2,1)S(1)} %all_to_all.10.rows_ref, bf16[512,512]{1,0:T(8,128)(2,1)S(1)} %get-tuple-element.29.x_ref, ...), custom_call_target="tpu_custom_call" | custom-call | tf_op jit(solution)/shard_map/whiten_own/pallas_call | solution.py:378
  61.0 0.2 collective-permute-done.3.inverse_ref
  61.3 0.9 whiten_other.1
  62.1 23.2 %all_to_all.11.bins_ref = bf16[32,8,1280]{2,1,0:T(8,128)(2,1)S(1)} all-to-all(bf16[32,8,1280]{2,1,0:T(8,128)(2,1)S(1)} %whiten_other.1), channel_id=1, replica_groups=mesh['samples_0'=8,'samples_1'=4,'samples_2'=2,'groups'=4] {'samples_0',..., dimensions={0} | all-to-all | bytes 1310720 | tf_op jit(solution)/shard_map/all_to_all | solution.py:489
  85.3 6.6 %restore.1 = bf16[16,20480]{1,0:T(8,128)(2,1)} custom-call(s32[1,20480]{1,0:T(1,128)S(1)} %get-tuple-element.24.code_ref, f32[5,32,128]{2,1,0:T(8,128)S(1)} %get-tuple-element.25.start_ref, bf16[4,256,5120]{2,1,0:T(8,128)(2,1)S(1)} %get-tuple-element.26.hot_ref, bf16[32,8,1280]{2,1,0:T(8,128)(2,1)S(1)} %all_to_all.11.bins_ref), custom_call_target="tpu_custom_call" | custom-call | tf_op jit(solution)/shard_map/restore/pallas_call | solution.py:378
  (3 shorter events, 0.0 us)
Async XLA Ops:
  0.0 0.9 copy-start.2
  0.9 1.1 %copy-start = (bf16[16,20480]{1,0:T(8,128)(2,1)S(1)}, bf16[16,20480]{1,0:T(8,128)(2,1)}, u32[]{:S(2)}) copy-start(bf16[16,20480]{1,0:T(8,128)(2,1)} %x_ref.1) | copy-start | bytes 1966084
  0.9 54.4 %copy-start.1 = (s32[64]{0:T(128)S(1)}, s32[64]{0:T(128)}, u32[]{:S(2)}) copy-start(s32[64]{0:T(128)} %sizes_ref.1) | copy-start | bytes 772
  40.9 4.5 %collective-permute-start = (bf16[32,8,1408]{2,1,0:T(8,128)(2,1)S(1)}, bf16[32,8,1408]{2,1,0:T(8,128)(2,1)S(1)}, u32[]{:S(2)}, u32[]{:S(2)}) collective-permute-start(bf16[32,8,1408]{2,1,0:T(8,128)(2,1)S(1)} %all_to_all.10.rows_ref), channel_id=1, source_target_pairs={{0,4},{4,0},{1,5},{5,1},{2,6},{6,2},{3,7},{7,3},{8,12},{12,8},{9,1... | collective-permute-start | bytes 2162696 | tf_op jit(solution)/shard_map/ppermute | solution.py:481
  46.3 4.1 %collective-permute-start.1 = (f32[8,128]{1,0:T(8,128)S(1)}, f32[8,128]{1,0:T(8,128)S(1)}, u32[]{:S(2)}, u32[]{:S(2)}) collective-permute-start(f32[8,128]{1,0:T(8,128)S(1)} %get-tuple-element.34.energy_ref), channel_id=1, source_target_pairs={{0,1},{1,0},{2,3},{3,2},{4,5},{5,4},{6,7},{7,6},{8,9},{9,8},{10,11... | collective-permute-start | bytes 12296 | tf_op jit(solution)/shard_map/ppermute | solution.py:485
  51.3 4.0 %collective-permute-start.2 = (f32[8,128]{1,0:T(8,128)S(1)}, f32[8,128]{1,0:T(8,128)S(1)}, u32[]{:S(2)}, u32[]{:S(2)}) collective-permute-start(f32[8,128]{1,0:T(8,128)S(1)} %get-tuple-element.35.e0_ref), channel_id=1, source_target_pairs={{0,2},{1,3},{2,0},{3,1},{4,6},{5,7},{6,4},{7,5},{8,10},{9,11},{10,... | collective-permute-start | bytes 12296 | tf_op jit(solution)/shard_map/ppermute | solution.py:485
  57.8 3.4 %collective-permute-start.3 = (bf16[512,512]{1,0:T(8,128)(2,1)S(1)}, bf16[512,512]{1,0:T(8,128)(2,1)S(1)}, u32[]{:S(2)}, u32[]{:S(2)}) collective-permute-start(bf16[512,512]{1,0:T(8,128)(2,1)S(1)} %inverse.1.inverse_ref), channel_id=1, source_target_pairs={{0,4},{4,0},{1,5},{5,1},{2,6},{6,2},{3,7},{7,3},{8,12},{12,8},{9,1... | collective-permute-start | bytes 1572872 | tf_op jit(solution)/shard_map/ppermute | solution.py:481

commit v4 on v3

--- a/solution.py
+++ b/solution.py
@@ -141,13 +141,14 @@
         masked(c, bin_row[:, columns], lhs_ref.at[c])
         runs.append(dot(lhs_ref[c], hot_ref[c], ((1,), (1,))))
 
-    total = jnp.zeros((8, LANES), F32)
+    sums = [jnp.zeros((rows, LANES), F32)] * 8
     for at in range(0, width, LANES):
         wide = x_ref[:, at : at + LANES].astype(F32)
-        square = wide * wide
-        for r in range(0, rows, 8):
-            total = total + square[r : r + 8]
-    total = whole(total, jnp.sum)
+        turn = at // LANES % len(sums)
+        sums[turn] = sums[turn] + wide * wide
+    while len(sums) > 1:
+        sums = [a + b for a, b in zip(sums[::2], sums[1::2])]
+    total = whole(sums[0], jnp.sum)
     first = total.astype(BF16).astype(F32)
     second = (total - first).astype(BF16).astype(F32)
     third = total - first - second

time: 92.8 us -> 92.6 us (level)
  no operation moved by 1% of the time
where the time goes in v4:
time: 92.6 us; the launch traced here: 91.8 us
  blocking collectives  55 us (59%)
  Pallas kernels  26.1 us (28%)
  starting transfers between devices  8.57 us (9%)
  waiting for transfers between devices  1.11 us (1%)
  local copies, waits for them, and re-layouts  0.97 us (1%)
    all_to_all x2, blocking collectives, exchange(): return lax.all_to_all(x, CHIPS, split_axis=0, concat_axis=0, tiled=True)  55 us
    pallas_call x11, Pallas kernels, on_core(): pl.pallas_call(kernel, grid=(1,), in_specs=[pl.BlockSpec(memory_space=plt...  26.1 us
    ppermute x2, starting transfers between devices, partner(): return lax.ppermute(x, 'samples_2', [(0, 1), (1, 0)])  4.54 us
    ppermute x2, starting transfers between devices, across(): lax.ppermute(x, 'groups', [(i, i ^ apart) for i in range(lax.axis_size('g...  4.03 us
  transfers between devices with their start and end apart: 4, of which 2 were waited for; matrix products, arithmetic and copies ran while one was open for 0% of the time, Pallas kernels for 7%

profile of v4, /device:TPU:1, one launch (start us, length us, event | category | flops | bytes accessed | tf_op | source)
XLA Modules:
  0.0 91.8 jit_solution(2318094269820749672)
XLA Ops:
  0.0 0.9 copy-done.2
  0.9 1.0 %places.1 = (s32[1,20480]{1,0:T(1,128)S(1)}, f32[5,32,128]{2,1,0:T(8,128)S(1)}) custom-call(s32[1,20480]{1,0:T(1,128)S(1)} %bitcast.2), custom_call_target="tpu_custom_call" | custom-call | flops 8000000000 | bytes 131072 | tf_op jit(solution)/shard_map/places/pallas_call | solution.py:379
  1.9 0.1 copy-done
  2.0 6.9 %partition.1 = (bf16[32,8,1408]{2,1,0:T(8,128)(2,1)S(1)}, f32[8,640]{1,0:T(8,128)S(1)}, bf16[4,256,5120]{2,1,0:T(8,128)(2,1)S(1)}) custom-call(s32[1]{0:T(128)} %bitcast.1.slot_ref, s32[1,20480]{1,0:T(1,128)S(1)} %get-tuple-element.24.code_ref, f32[5,32,128]{2,1,0:T(8,128)S(1)} %get-tuple-element.25.start_ref, bf16[16,20480]{1,0:T(8,128)(2,1)S(1)} %copy-done), custom_call_target="tpu_custom_call" | custom-call | tf_op jit(solution)/shard_map/partition/pallas_call | solution.py:379
  8.9 31.8 %all_to_all.10.rows_ref = bf16[32,8,1408]{2,1,0:T(8,128)(2,1)S(1)} all-to-all(bf16[32,8,1408]{2,1,0:T(8,128)(2,1)S(1)} %get-tuple-element.28), channel_id=1, replica_groups=mesh['samples_0'=8,'samples_1'=4,'samples_2'=2,'groups'=4] {'samples_0',..., dimensions={0} | all-to-all | bytes 1441792 | tf_op jit(solution)/shard_map/all_to_all | solution.py:490
  40.7 2.7 %collective-permute-start = (bf16[32,8,1408]{2,1,0:T(8,128)(2,1)S(1)}, bf16[32,8,1408]{2,1,0:T(8,128)(2,1)S(1)}, u32[]{:S(2)}, u32[]{:S(2)}) collective-permute-start(bf16[32,8,1408]{2,1,0:T(8,128)(2,1)S(1)} %all_to_all.10.rows_ref), channel_id=1, source_target_pairs={{0,4},{4,0},{1,5},{5,1},{2,6},{6,2},{3,7},{7,3},{8,12},{12,8},{9,1... | collective-permute-start | bytes 2162696 | tf_op jit(solution)/shard_map/ppermute | solution.py:482
  43.4 0.9 %gram_own.1 = (f32[512,512]{1,0:T(8,128)S(1)}, bf16[512,512]{1,0:T(8,128)(2,1)S(1)}, f32[8,128]{1,0:T(8,128)S(1)}) custom-call(s32[1]{0:T(128)} %bitcast.1.slot_ref, f32[8,640]{1,0:T(8,128)S(1)} %get-tuple-element.27.places_ref, bf16[32,8,1408]{2,1,0:T(8,128)(2,1)S(1)} %all_to_all.10.rows_ref), custom_call_target="tpu_custom_call" | custom-call | tf_op jit(solution)/shard_map/gram_own/pallas_call | solution.py:379
  44.3 0.9 collective-permute-done.rows_ref
  45.2 0.9 %gram_other.1 = (f32[512,512]{1,0:T(8,128)S(1)}, f32[8,128]{1,0:T(8,128)S(1)}) custom-call(s32[1]{0:T(128)} %bitcast.1.slot_ref, f32[8,640]{1,0:T(8,128)S(1)} %get-tuple-element.27.places_ref, bf16[32,8,1408]{2,1,0:T(8,128)(2,1)S(1)} %collective-permute-done.rows_ref, f32[512,512]{1,0:T(8,128)S(1)} %get-tuple-element.30.before_ref, ...), custom_call_target="tpu_custom_call" | custom-call | tf_op jit(solution)/shard_map/gram_other/pallas_call | solution.py:379
  46.2 1.5 %collective-permute-start.1 = (f32[8,128]{1,0:T(8,128)S(1)}, f32[8,128]{1,0:T(8,128)S(1)}, u32[]{:S(2)}, u32[]{:S(2)}) collective-permute-start(f32[8,128]{1,0:T(8,128)S(1)} %get-tuple-element.34.energy_ref), channel_id=1, source_target_pairs={{0,1},{1,0},{2,3},{3,2},{4,5},{5,4},{6,7},{7,6},{8,9},{9,8},{10,11... | collective-permute-start | bytes 12296 | tf_op jit(solution)/shard_map/ppermute | solution.py:486
  47.6 2.6 %first_powers.1 = (f32[3,512,512]{2,1,0:T(8,128)S(1)}, f32[512,512]{1,0:T(8,128)S(1)}, f32[8,128]{1,0:T(8,128)S(1)}) custom-call(f32[512,512]{1,0:T(8,128)S(1)} %get-tuple-element.32.gram_ref), custom_call_target="tpu_custom_call" | custom-call | tf_op jit(solution)/shard_map/first_powers/pallas_call | solution.py:379
  50.2 0.0 collective-permute-done.1.neighbour_ref
  50.2 0.9 eighth_power.1
  51.1 2.5 %collective-permute-start.2 = (f32[8,128]{1,0:T(8,128)S(1)}, f32[8,128]{1,0:T(8,128)S(1)}, u32[]{:S(2)}, u32[]{:S(2)}) collective-permute-start(f32[8,128]{1,0:T(8,128)S(1)} %get-tuple-element.35.e0_ref), channel_id=1, source_target_pairs={{0,2},{1,3},{2,0},{3,1},{4,6},{5,7},{6,4},{7,5},{8,10},{9,11},{10,... | collective-permute-start | bytes 12296 | tf_op jit(solution)/shard_map/ppermute | solution.py:486
  53.6 1.5 %last_powers.1 = (f32[512,512]{1,0:T(8,128)S(1)}, bf16[2,512,512]{2,1,0:T(8,128)(2,1)S(1)}) custom-call(f32[512,512]{1,0:T(8,128)S(1)} %get-tuple-element.33.fourth_ref, f32[512,512]{1,0:T(8,128)S(1)} %get-tuple-element.38.eighth_ref), custom_call_target="tpu_custom_call" | custom-call | tf_op jit(solution)/shard_map/last_powers/pallas_call | solution.py:379
  55.2 0.0 collective-permute-done.2.e1_ref
  55.2 0.0 copy-done.1
  55.2 2.5 %inverse.1.inverse_ref = bf16[512,512]{1,0:T(8,128)(2,1)S(1)} custom-call(s32[1]{0:T(128)} %bitcast.1.slot_ref, s32[64]{0:T(128)S(1)} %copy-done.1, f32[8,128]{1,0:T(8,128)S(1)} %get-tuple-element.35.e0_ref, f32[8,128]{1,0:T(8,128)S(1)} %collective-permute-done.2.e1_ref, f32[8,128]{1,0:T(8,128)S(1)} %get-tuple-element.36.sums_ref, ...), custom_call_target="tpu_custom_call" | custom-call | tf_op jit(solution)/shard_map/inverse/pallas_call | solution.py:379
  57.7 1.9 %collective-permute-start.3 = (bf16[512,512]{1,0:T(8,128)(2,1)S(1)}, bf16[512,512]{1,0:T(8,128)(2,1)S(1)}, u32[]{:S(2)}, u32[]{:S(2)}) collective-permute-start(bf16[512,512]{1,0:T(8,128)(2,1)S(1)} %inverse.1.inverse_ref), channel_id=1, source_target_pairs={{0,4},{4,0},{1,5},{5,1},{2,6},{6,2},{3,7},{7,3},{8,12},{12,8},{9,1... | collective-permute-start | bytes 1572872 | tf_op jit(solution)/shard_map/ppermute | solution.py:482
  59.6 1.3 %whiten_own.1 = (bf16[512,640]{1,0:T(8,128)(2,1)S(1)}, bf16[512,512]{1,0:T(8,128)(2,1)S(1)}) custom-call(s32[1]{0:T(128)} %bitcast.1.slot_ref, f32[8,640]{1,0:T(8,128)S(1)} %get-tuple-element.27.places_ref, bf16[32,8,1408]{2,1,0:T(8,128)(2,1)S(1)} %all_to_all.10.rows_ref, bf16[512,512]{1,0:T(8,128)(2,1)S(1)} %get-tuple-element.29.x_ref, ...), custom_call_target="tpu_custom_call" | custom-call | tf_op jit(solution)/shard_map/whiten_own/pallas_call | solution.py:379
  60.9 0.2 collective-permute-done.3.inverse_ref
  61.1 0.9 whiten_other.1
  62.0 23.2 %all_to_all.11.bins_ref = bf16[32,8,1280]{2,1,0:T(8,128)(2,1)S(1)} all-to-all(bf16[32,8,1280]{2,1,0:T(8,128)(2,1)S(1)} %whiten_other.1), channel_id=1, replica_groups=mesh['samples_0'=8,'samples_1'=4,'samples_2'=2,'groups'=4] {'samples_0',..., dimensions={0} | all-to-all | bytes 1310720 | tf_op jit(solution)/shard_map/all_to_all | solution.py:490
  85.2 6.6 %restore.1 = bf16[16,20480]{1,0:T(8,128)(2,1)} custom-call(s32[1,20480]{1,0:T(1,128)S(1)} %get-tuple-element.24.code_ref, f32[5,32,128]{2,1,0:T(8,128)S(1)} %get-tuple-element.25.start_ref, bf16[4,256,5120]{2,1,0:T(8,128)(2,1)S(1)} %get-tuple-element.26.hot_ref, bf16[32,8,1280]{2,1,0:T(8,128)(2,1)S(1)} %all_to_all.11.bins_ref), custom_call_target="tpu_custom_call" | custom-call | tf_op jit(solution)/shard_map/restore/pallas_call | solution.py:379
  (3 shorter events, 0.0 us)
Async XLA Ops:
  0.0 0.9 copy-start.2
  0.9 1.1 %copy-start = (bf16[16,20480]{1,0:T(8,128)(2,1)S(1)}, bf16[16,20480]{1,0:T(8,128)(2,1)}, u32[]{:S(2)}) copy-start(bf16[16,20480]{1,0:T(8,128)(2,1)} %x_ref.1) | copy-start | bytes 1966084
  0.9 54.3 %copy-start.1 = (s32[64]{0:T(128)S(1)}, s32[64]{0:T(128)}, u32[]{:S(2)}) copy-start(s32[64]{0:T(128)} %sizes_ref.1) | copy-start | bytes 772
  40.7 4.5 %collective-permute-start = (bf16[32,8,1408]{2,1,0:T(8,128)(2,1)S(1)}, bf16[32,8,1408]{2,1,0:T(8,128)(2,1)S(1)}, u32[]{:S(2)}, u32[]{:S(2)}) collective-permute-start(bf16[32,8,1408]{2,1,0:T(8,128)(2,1)S(1)} %all_to_all.10.rows_ref), channel_id=1, source_target_pairs={{0,4},{4,0},{1,5},{5,1},{2,6},{6,2},{3,7},{7,3},{8,12},{12,8},{9,1... | collective-permute-start | bytes 2162696 | tf_op jit(solution)/shard_map/ppermute | solution.py:482
  46.2 4.1 %collective-permute-start.1 = (f32[8,128]{1,0:T(8,128)S(1)}, f32[8,128]{1,0:T(8,128)S(1)}, u32[]{:S(2)}, u32[]{:S(2)}) collective-permute-start(f32[8,128]{1,0:T(8,128)S(1)} %get-tuple-element.34.energy_ref), channel_id=1, source_target_pairs={{0,1},{1,0},{2,3},{3,2},{4,5},{5,4},{6,7},{7,6},{8,9},{9,8},{10,11... | collective-permute-start | bytes 12296 | tf_op jit(solution)/shard_map/ppermute | solution.py:486
  51.1 4.1 %collective-permute-start.2 = (f32[8,128]{1,0:T(8,128)S(1)}, f32[8,128]{1,0:T(8,128)S(1)}, u32[]{:S(2)}, u32[]{:S(2)}) collective-permute-start(f32[8,128]{1,0:T(8,128)S(1)} %get-tuple-element.35.e0_ref), channel_id=1, source_target_pairs={{0,2},{1,3},{2,0},{3,1},{4,6},{5,7},{6,4},{7,5},{8,10},{9,11},{10,... | collective-permute-start | bytes 12296 | tf_op jit(solution)/shard_map/ppermute | solution.py:486
  57.7 3.4 %collective-permute-start.3 = (bf16[512,512]{1,0:T(8,128)(2,1)S(1)}, bf16[512,512]{1,0:T(8,128)(2,1)S(1)}, u32[]{:S(2)}, u32[]{:S(2)}) collective-permute-start(bf16[512,512]{1,0:T(8,128)(2,1)S(1)} %inverse.1.inverse_ref), channel_id=1, source_target_pairs={{0,4},{4,0},{1,5},{5,1},{2,6},{6,2},{3,7},{7,3},{8,12},{12,8},{9,1... | collective-permute-start | bytes 1572872 | tf_op jit(solution)/shard_map/ppermute | solution.py:482
